TPU v7x, 32 devices: a whole 2x2x4 slice. The times are simulated.
32 devices in a mesh: groups: 2 (over x), tok: 16 (over z, y, core).
Axes of the slice: x: 2, y: 2, z: 4, core: 2. Of those that a mesh axis runs over, the one named last changes fastest.
Arguments:
- tokens: bfloat16 [4, 8192, 512], P('groups', 'tok'), parts along dimension 0, may hold values from -28 to 28
- w_query: bfloat16 [512, 512], replicated, may hold values from -0.25 to 0.25
- w_key: bfloat16 [512, 512], replicated, may hold values from -0.25 to 0.25
- w_value: bfloat16 [512, 512], replicated, may hold values from -0.25 to 0.25
- w_out: bfloat16 [512, 512], replicated, may hold values from -0.25 to 0.25
- partner_block: int32 [16, 4], P('tok'), may hold values from 0 to 3
- head_masks: int32 [16, 4, 8], P('tok'), may hold values 0 or 1
- cotangent: bfloat16 [4, 8192, 512], P('groups', 'tok'), parts along dimension 0, may hold values from -6 to 6
Outputs:
- output: bfloat16 [4, 8192, 512], P('groups', 'tok'), parts along dimension 0
- grad_tokens: bfloat16 [4, 8192, 512], P('groups', 'tok'), parts along dimension 0
- grad_query: float32 [1024, 512], P('groups'), parts along dimension 0
- grad_key: float32 [1024, 512], P('groups'), parts along dimension 0
- grad_value: float32 [1024, 512], P('groups'), parts along dimension 0
- grad_out: float32 [1024, 512], P('groups'), parts along dimension 0
There are 2 independent parts, one for each index of `groups`. A program takes and returns all parts, laid end to end along the dimension named above; an argument that names none is the same for every part. Nothing has to cross between parts.
All inputs are finite; a program needn't handle non-finite values. No bound on the sum of `head_masks` on one device may be relied on, other than what follows from the above.
Results may differ from a plain program's by a relative error of at most 0.015.
The roundings to bfloat16 on the way count: a program that leaves them out, or rounds other values in their place, can miss the bound.
Values may be sent and summed in bfloat16 or wider, within the bound.
A program may use at most 128 MiB of HBM per device.

v0:
```python
import math

import jax
import jax.numpy as jnp
from jax import lax
from jax.sharding import PartitionSpec as P

SUB = 128


def partner(x, axis, stride):
    return lax.ppermute(x, axis, [(i, i ^ 1 << stride) for i in range(lax.axis_size(axis))])


def attend(queries, gathered, mask_rows, grad_output, w_out, score_scale):
    samples, block_rows, model_width = queries.shape
    head_count = mask_rows.shape[1]
    head_width = model_width // head_count
    key_count = gathered.shape[1]
    sub_rows = (key_count - block_rows) // 4
    f32 = jnp.float32
    query_heads = queries.reshape(samples, block_rows, head_count, head_width)
    key_heads = gathered[..., :model_width].reshape(samples, key_count, head_count, head_width)
    value_heads = gathered[..., model_width:].reshape(samples, key_count, head_count, head_width)
    visible = (
        jnp.concatenate(
            [
                jnp.ones((head_count, block_rows), jnp.int32),
                jnp.repeat(mask_rows.T, sub_rows, axis=1),
            ],
            1,
        )
        > 0
    )
    scores = (
        jnp.einsum("sqhd,skhd->shqk", query_heads, key_heads, preferred_element_type=f32)
        * score_scale
    )
    scores = jnp.where(visible[None, :, None, :], scores, -jnp.inf)
    row_max = jnp.max(scores, axis=-1, keepdims=True)
    expo_terms = jnp.exp(scores - row_max)
    probability = expo_terms / jnp.sum(expo_terms, axis=-1, keepdims=True)
    prob_half = probability.astype(jnp.bfloat16)
    context = jnp.einsum(
        "shqk,skhd->sqhd", prob_half, value_heads, preferred_element_type=f32
    ).astype(jnp.bfloat16)
    context_rows = context.reshape(samples * block_rows, model_width)
    output = jnp.dot(context_rows, w_out, preferred_element_type=f32).astype(jnp.bfloat16)
    grad_rows = grad_output.reshape(samples * block_rows, model_width)
    grad_context = jnp.dot(grad_rows, w_out.T, preferred_element_type=f32).astype(jnp.bfloat16)
    grad_context = grad_context.reshape(samples, block_rows, head_count, head_width)
    grad_prob = jnp.einsum("sqhd,skhd->shqk", grad_context, value_heads, preferred_element_type=f32)
    row_dot = jnp.sum(grad_context.astype(f32) * context.astype(f32), axis=-1).transpose(0, 2, 1)
    grad_score = (probability * (grad_prob - row_dot[..., None]) * score_scale).astype(jnp.bfloat16)
    grad_q = jnp.einsum(
        "shqk,skhd->sqhd", grad_score, key_heads, preferred_element_type=f32
    ).astype(jnp.bfloat16)
    grad_k = jnp.einsum("shqk,sqhd->skhd", grad_score, query_heads, preferred_element_type=f32)
    grad_v = jnp.einsum("shqk,sqhd->skhd", prob_half, grad_context, preferred_element_type=f32)
    key_grads = jnp.concatenate(
        [
            grad_k.reshape(samples, key_count, model_width),
            grad_v.reshape(samples, key_count, model_width),
        ],
        -1,
    )
    return (
        output.reshape(samples, block_rows, model_width),
        context_rows.reshape(samples, block_rows, model_width),
        grad_q.reshape(samples, block_rows, model_width),
        key_grads,
    )


def per_device(tokens, w_query, w_key, w_value, w_out, partner_block, head_masks, cotangent):
    f32 = jnp.float32
    samples, block_rows, model_width = tokens.shape
    levels = lax.axis_size("tok").bit_length() - 1
    sub_rows = SUB
    score_scale = 1.0 / math.sqrt(model_width // head_masks.shape[2])
    sent_starts = []
    for section in range(4):
        theirs = partner(partner_block, "tok", levels - 4 + section)
        sent_starts.append(theirs[0, section] * sub_rows)
    token_rows = tokens.reshape(samples * block_rows, model_width)
    queries = (
        jnp.dot(token_rows, w_query, preferred_element_type=f32)
        .astype(jnp.bfloat16)
        .reshape(samples, block_rows, model_width)
    )
    w_key_value = jnp.concatenate([w_key, w_value], 1)
    key_value = (
        jnp.dot(token_rows, w_key_value, preferred_element_type=f32)
        .astype(jnp.bfloat16)
        .reshape(samples, block_rows, 2 * model_width)
    )
    pieces = [key_value]
    for section in range(4):
        bit_number = levels - 4 + section
        chosen = lax.dynamic_slice_in_dim(tokens, sent_starts[section], sub_rows, 1)
        arrived = partner(chosen, "tok", bit_number)
        projected = jnp.dot(
            arrived.reshape(samples * sub_rows, model_width),
            w_key_value,
            preferred_element_type=f32,
        )
        pieces.append(projected.astype(jnp.bfloat16).reshape(samples, sub_rows, 2 * model_width))
    gathered = jnp.concatenate(pieces, 1)
    results = [
        attend(
            queries[sample : sample + 1],
            gathered[sample : sample + 1],
            head_masks[0],
            cotangent[sample : sample + 1],
            w_out,
            score_scale,
        )
        for sample in range(samples)
    ]
    output = jnp.concatenate([item[0] for item in results], 0)
    context = jnp.concatenate([item[1] for item in results], 0)
    grad_q = jnp.concatenate([item[2] for item in results], 0)
    key_grads = jnp.concatenate([item[3] for item in results], 0)
    own_grads = key_grads[:, :block_rows]
    for section in range(4):
        bit_number = levels - 4 + section
        first_row = block_rows + section * sub_rows
        part_grad = key_grads[:, first_row : first_row + sub_rows]
        returned = partner(part_grad, "tok", bit_number)
        current = lax.dynamic_slice_in_dim(own_grads, sent_starts[section], sub_rows, 1)
        own_grads = lax.dynamic_update_slice_in_dim(
            own_grads, current + returned, sent_starts[section], 1
        )
    grad_q_rows = grad_q.reshape(samples * block_rows, model_width)
    grad_kv_rows = own_grads.astype(jnp.bfloat16).reshape(samples * block_rows, 2 * model_width)
    grad_tokens = (
        jnp.dot(grad_q_rows, w_query.T, preferred_element_type=f32)
        + jnp.dot(grad_kv_rows, w_key_value.T, preferred_element_type=f32)
    ).astype(jnp.bfloat16)
    grad_query = jnp.dot(token_rows.T, grad_q_rows, preferred_element_type=f32)
    grad_pair = jnp.dot(token_rows.T, grad_kv_rows, preferred_element_type=f32)
    grad_out = jnp.dot(
        context.reshape(samples * block_rows, model_width).T,
        cotangent.reshape(samples * block_rows, model_width),
        preferred_element_type=f32,
    )
    summed = lax.psum(
        (grad_query, grad_pair[:, :model_width], grad_pair[:, model_width:], grad_out), "tok"
    )
    return (
        output,
        grad_tokens.reshape(samples, block_rows, model_width),
        summed[0],
        summed[1],
        summed[2],
        summed[3],
    )


def solution(mesh):
    placed = (
        P("groups", "tok", None),
        P(),
        P(),
        P(),
        P(),
        P("tok", None),
        P("tok", None, None),
        P("groups", "tok", None),
    )
    return jax.shard_map(
        per_device,
        mesh=mesh,
        in_specs=placed,
        out_specs=(
            P("groups", "tok", None),
            P("groups", "tok", None),
            P("groups", None),
            P("groups", None),
            P("groups", None),
            P("groups", None),
        ),
        check_vma=False,
    )
```

profile of v0, /device:TPU:0, one launch (start us, length us, event | category | flops | bytes accessed | tf_op | source)
XLA Modules:
  0.0 336.1 jit_solution(179325345437837072)
XLA Ops:
  7.2 3.1 collective-permute-start.2
  10.3 2.6 collective-permute-start.6
  12.9 1.6 collective-permute-start.4
  14.5 1.5 convolution_convert_fusion.5
  16.0 2.3 convolution_convert_fusion.3
  18.3 0.8 broadcast_bitcast_fusion
  19.1 1.1 constant_dynamic-update-slice_fusion.1
  20.2 1.1 constant_dynamic-update-slice_fusion
  21.3 3.1 convolution_convert_fusion.1
  24.4 1.3 convolution_convert_fusion
  25.6 1.5 constant_dynamic-update-slice_fusion.6
  27.1 0.6 slice.66
  28.4 0.6 slice.68
  31.4 2.5 fusion.34
  34.5 11.3 %collective-permute-done.7 = bf16[2,128,512]{2,1,0:T(8,128)(2,1)S(1)} collective-permute-done((bf16[2,128,512]{2,1,0:T(8,128)(2,1)S(1)}, bf16[2,128,512]{2,1,0:T(8,128)(2,1)S(1)}, u32[]{:S(2)}, u32[]{:S(2)}) %collective-permute-start.7) | collective-permute-done | bytes 262176 | tf_op jit(solution)/shard_map/ppermute | solution.py:12
  46.2 1.0 collective-permute-done.5
  48.8 2.1 fusion.32
  50.9 1.6 copy.24
  52.5 2.3 copy.23
  54.8 9.4 %fusion.35 = (f32[8,512]{1,0:T(8,128)S(1)}, f32[8,512,1024]{2,1,0:T(8,128)}) fusion(pred[8,1024]{1,0:T(8,128)(4,1)S(1)} %pad_compare_fusion, bf16[512,8,64]{0,2,1:T(8,128)(2,1)} %bitcast.188, bf16[1024,8,64]{0,2,1:T(8,128)(2,1)S(1)} %bitcast.173), kind=kOutput, calls=%fused_computation.85 | convolution fusion | flops 553649152 | bytes 18374656 | tf_op jit(solution)/shard_map/sub | solution.py:41
  64.2 7.0 %fusion.11 = bf16[8,512,1024]{2,1,0:T(8,128)(2,1)S(1)} fusion(f32[8,512,1024]{2,1,0:T(8,128)} %get-tuple-element.39, f32[8,512]{1,0:T(8,128)S(1)} %get-tuple-element.38), kind=kLoop, calls=%fused_computation.20 | loop fusion | flops 8388608 | bytes 25182208 | tf_op jit(solution)/shard_map/convert_element_type | solution.py:43
  71.2 2.9 fusion.41
  74.1 3.5 %fusion.17 = (f32[512,8]{0,1:T(8,128)S(1)}, bf16[8,64,512]{2,1,0:T(8,128)(2,1)}) fusion(bf16[1,512,8,64]{1,3,2,0:T(8,128)(2,1)S(1)} %bitcast.184, bf16[1024,8,64]{0,2,1:T(8,128)(2,1)S(1)} %bitcast.177, bf16[8,512,1024]{2,1,0:T(8,128)(2,1)S(1)} %fusion.11), kind=kOutput, calls=%fused_computation.51 | convolution fusion | flops 538177536 | bytes 10502144 | tf_op jit(solution)/shard_map/shqk,skhd->sqhd/dot_general | solution.py:44
  77.6 7.6 %multiply_convert_fusion = bf16[8,512,1024]{2,1,0:T(8,128)(2,1)S(1)} fusion(bf16[512,8,64]{0,2,1:T(8,128)(2,1)S(1)} %bitcast.185, bf16[1024,8,64]{0,2,1:T(8,128)(2,1)S(1)} %bitcast.178, f32[8,512]{1,0:T(8,128)S(1)} %bitcast.210, f32[8,512,1024]{2,1,0:T(8,128)} %get-tuple-element.39, f32[8,512]{1,0:T(8,128)S(1)} %get-tuple-element.38), kind=kOutput, calls=%fused_computation.2 | convolution fusion | flops 557842432 | bytes 26771456 | tf_op jit(solution)/shard_map/sqhd,skhd->shqk/dot_general | solution.py:52
  85.2 3.5 %convolution_convert_fusion.2 = bf16[8,64,512]{2,1,0:T(8,128)(2,1)} fusion(bf16[1024,8,64]{0,2,1:T(8,128)(2,1)S(1)} %bitcast.174, bf16[8,512,1024]{2,1,0:T(8,128)(2,1)S(1)} %multiply_convert_fusion), kind=kOutput, calls=%fused_computation.27 | convolution fusion | flops 537133056 | bytes 9961472 | tf_op jit(solution)/shard_map/shqk,skhd->sqhd/dot_general | solution.py:55
  88.7 2.9 fusion.40
  91.6 1.5 copy.22
  93.1 2.3 copy.21
  95.3 3.1 copy.28
  98.4 2.9 copy.29
  101.3 9.4 %fusion.36 = (f32[8,512]{1,0:T(8,128)S(1)}, f32[8,512,1024]{2,1,0:T(8,128)}) fusion(pred[8,1024]{1,0:T(8,128)(4,1)S(1)} %pad_compare_fusion, bf16[512,8,64]{0,2,1:T(8,128)(2,1)} %bitcast.186, bf16[1024,8,64]{0,2,1:T(8,128)(2,1)S(1)} %bitcast.171), kind=kOutput, calls=%fused_computation.86 | convolution fusion | flops 553649152 | bytes 18374656 | tf_op jit(solution)/shard_map/sub | solution.py:41
  110.7 7.0 %fusion.10 = bf16[8,512,1024]{2,1,0:T(8,128)(2,1)S(1)} fusion(f32[8,512,1024]{2,1,0:T(8,128)} %get-tuple-element.41, f32[8,512]{1,0:T(8,128)S(1)} %get-tuple-element.40), kind=kLoop, calls=%fused_computation.19 | loop fusion | flops 8388608 | bytes 25182208 | tf_op jit(solution)/shard_map/convert_element_type | solution.py:43
  117.7 2.9 fusion.39
  120.6 3.5 %fusion.18 = (f32[512,8]{0,1:T(8,128)S(1)}, bf16[8,64,512]{2,1,0:T(8,128)(2,1)}) fusion(bf16[1,512,8,64]{1,3,2,0:T(8,128)(2,1)S(1)} %bitcast.181, bf16[1024,8,64]{0,2,1:T(8,128)(2,1)S(1)} %bitcast.175, bf16[8,512,1024]{2,1,0:T(8,128)(2,1)S(1)} %fusion.10), kind=kOutput, calls=%fused_computation.53 | convolution fusion | flops 538177536 | bytes 10502144 | tf_op jit(solution)/shard_map/shqk,skhd->sqhd/dot_general | solution.py:44
  124.1 7.7 %multiply_convert_fusion.1 = bf16[8,512,1024]{2,1,0:T(8,128)(2,1)S(1)} fusion(bf16[512,8,64]{0,2,1:T(8,128)(2,1)S(1)} %bitcast.182, bf16[1024,8,64]{0,2,1:T(8,128)(2,1)S(1)} %bitcast.176, f32[8,512]{1,0:T(8,128)S(1)} %bitcast.211, f32[8,512,1024]{2,1,0:T(8,128)} %get-tuple-element.41, f32[8,512]{1,0:T(8,128)S(1)} %get-tuple-element.40), kind=kOutput, calls=%fused_computation.3 | convolution fusion | flops 557842432 | bytes 26771456 | tf_op jit(solution)/shard_map/sqhd,skhd->shqk/dot_general | solution.py:52
  131.8 3.3 copy-done.1
  135.0 2.9 fusion.38
  137.9 3.0 copy.26
  140.9 3.1 copy.27
  144.1 2.8 maximum_maximum_fusion.1
  147.0 6.8 %convolution_convert_fusion.4 = bf16[8,64,512]{2,1,0:T(8,128)(2,1)S(1)} fusion(bf16[1024,8,64]{0,2,1:T(8,128)(2,1)S(1)} %bitcast.172, bf16[8,512,1024]{2,1,0:T(8,128)(2,1)} %copy-done.1), kind=kOutput, calls=%fused_computation.29 | convolution fusion | flops 537133056 | bytes 9961472 | tf_op jit(solution)/shard_map/shqk,skhd->sqhd/dot_general | solution.py:55
  154.4 0.9 maximum_maximum_fusion
  155.7 1.8 collective-permute-start.11
  157.6 1.7 convolution_bitcast_fusion.1
  159.3 1.7 convolution_bitcast_fusion.2
  161.0 1.4 add_dynamic-update-slice_fusion.3
  162.4 16.3 %collective-permute-done.9 = f32[2,128,1024]{2,1,0:T(8,128)S(1)} collective-permute-done((f32[2,128,1024]{2,1,0:T(8,128)S(1)}, f32[2,128,1024]{2,1,0:T(8,128)S(1)}, u32[]{:S(2)}, u32[]{:S(2)}) %collective-permute-start.9) | collective-permute-done | bytes 1048608 | tf_op jit(solution)/shard_map/ppermute | solution.py:12
  178.9 19.2 %collective-permute-done.10 = f32[2,128,1024]{2,1,0:T(8,128)S(1)} collective-permute-done((f32[2,128,1024]{2,1,0:T(8,128)S(1)}, f32[2,128,1024]{2,1,0:T(8,128)S(1)}, u32[]{:S(2)}, u32[]{:S(2)}) %collective-permute-start.10) | collective-permute-done | bytes 1048608 | tf_op jit(solution)/shard_map/ppermute | solution.py:12
  198.3 5.4 %collective-permute-done.11 = f32[2,128,1024]{2,1,0:T(8,128)S(1)} collective-permute-done((f32[2,128,1024]{2,1,0:T(8,128)S(1)}, f32[2,128,1024]{2,1,0:T(8,128)S(1)}, u32[]{:S(2)}, u32[]{:S(2)}) %collective-permute-start.11) | collective-permute-done | bytes 1048608 | tf_op jit(solution)/shard_map/ppermute | solution.py:12
  204.3 1.3 copy-done.12
  205.6 1.3 convolution_bitcast_fusion
  206.9 1.5 fusion.33
  208.4 1.1 pad_maximum_fusion.1
  209.4 1.5 copy.25
  211.0 1.6 fusion.13
  212.6 1.7 fusion.12
  214.3 1.1 pad_maximum_fusion
  215.3 1.8 fusion.37
  217.1 2.3 add_convert_fusion
  219.4 99.6 %all-reduce.4.cloned.1.call-done = (f32[512,512]{0,1:T(8,128)}, f32[512,512]{0,1:T(8,128)}, f32[512,512]{0,1:T(8,128)}, f32[512,512]{1,0:T(8,128)}) async-done(((f32[512,512]{0,1:T(8,128)}, f32[512,512]{0,1:T(8,128)}, f32[512,512]{0,1:T(8,128)}, f32[512,512]{1,0:T(8,128)}), (f32[512,512]{0,1:T(8,128)}, f32[512,512]{0,1:T(8,128)}, f32[512,512]{0,1:T(8,128)}, ...) | async-done | bytes 4194320 | tf_op jit(solution)/shard_map/psum | solution.py:147
  318.9 2.5 copy.31
  321.5 2.5 copy.32
  324.0 2.5 copy.33
  326.5 2.3 copy.48
  (71 shorter events, 5.7 us)
Async XLA Ops:
  7.2 7.3 %copy-start = (bf16[512,512]{1,0:T(8,128)(2,1)S(1)}, bf16[512,512]{1,0:T(8,128)(2,1)}, u32[]{:S(2)}) copy-start(bf16[512,512]{1,0:T(8,128)(2,1)} %param.12) | copy-start | bytes 1572868
  7.2 17.2 %copy-start.15 = (bf16[2,512,512]{2,1,0:T(8,128)(2,1)S(1)}, bf16[2,512,512]{2,1,0:T(8,128)(2,1)}, u32[]{:S(2)}) copy-start(bf16[2,512,512]{2,1,0:T(8,128)(2,1)} %param.8) | copy-start | bytes 3145732
  7.2 311.8 %all-reduce.4.cloned.1.call-start = ((), (), s32[]{:S(2)}) async-start(), calls=%async_computation | async-start | bytes 8388608 | tf_op jit(solution)/shard_map/psum | solution.py:147
  7.2 19.9 %collective-permute-start.2 = (s32[1,4]{1,0:T(1,128)}, s32[1,4]{1,0:T(1,128)S(1)}, u32[]{:S(2)}, u32[]{:S(2)}) collective-permute-start(s32[1,4]{1,0:T(1,128)} %param.13), channel_id=1, source_target_pairs={{0,2},{1,3},{2,0},{3,1},{4,6},{5,7},{6,4},{7,5},{8,10},{9,11},{10,... | collective-permute-start | bytes 56 | tf_op jit(solution)/shard_map/ppermute | solution.py:12
  10.3 18.1 %collective-permute-start = (s32[1,4]{1,0:T(1,128)}, s32[1,4]{1,0:T(1,128)S(1)}, u32[]{:S(2)}, u32[]{:S(2)}) collective-permute-start(s32[1,4]{1,0:T(1,128)} %param.13), channel_id=1, source_target_pairs={{0,1},{1,0},{2,3},{3,2},{4,5},{5,4},{6,7},{7,6},{8,9},{9,8},{10,11... | collective-permute-start | bytes 56 | tf_op jit(solution)/shard_map/ppermute | solution.py:12
  10.3 18.1 %collective-permute-start.6 = (s32[1,4]{1,0:T(1,128)}, s32[1,4]{1,0:T(1,128)S(1)}, u32[]{:S(2)}, u32[]{:S(2)}) collective-permute-start(s32[1,4]{1,0:T(1,128)} %param.13), channel_id=1, source_target_pairs={{0,8},{1,9},{2,10},{3,11},{4,12},{5,13},{6,14},{7,15},{8,0},{9,1},... | collective-permute-start | bytes 56 | tf_op jit(solution)/shard_map/ppermute | solution.py:12
  12.9 16.8 %collective-permute-start.4 = (s32[1,4]{1,0:T(1,128)}, s32[1,4]{1,0:T(1,128)S(1)}, u32[]{:S(2)}, u32[]{:S(2)}) collective-permute-start(s32[1,4]{1,0:T(1,128)} %param.13), channel_id=1, source_target_pairs={{0,4},{1,5},{2,6},{3,7},{4,0},{5,1},{6,2},{7,3},{8,12},{9,13},{10,... | collective-permute-start | bytes 56 | tf_op jit(solution)/shard_map/ppermute | solution.py:12
  30.9 17.7 %copy-start.6 = (bf16[2,1024,1024]{2,1,0:T(8,128)(2,1)S(1)}, bf16[2,1024,1024]{2,1,0:T(8,128)(2,1)}, u32[]{:S(2)}) copy-start(bf16[2,1024,1024]{2,1,0:T(8,128)(2,1)} %constant_dynamic-update-slice_fusion.6) | copy-start | bytes 12582916
  31.0 14.7 %collective-permute-start.7 = (bf16[2,128,512]{2,1,0:T(8,128)(2,1)S(1)}, bf16[2,128,512]{2,1,0:T(8,128)(2,1)S(1)}, u32[]{:S(2)}, u32[]{:S(2)}) collective-permute-start(bf16[2,128,512]{2,1,0:T(8,128)(2,1)S(1)} %get-tuple-element.34), channel_id=1, source_target_pairs={{0,8},{1,9},{2,10},{3,11},{4,12},{5,13},{6,14},{7,15},{8,0},{9,1},... | collective-permute-start | bytes 786440 | tf_op jit(solution)/shard_map/ppermute | solution.py:12
  33.9 13.3 %collective-permute-start.5 = (bf16[2,128,512]{2,1,0:T(8,128)(2,1)S(1)}, bf16[2,128,512]{2,1,0:T(8,128)(2,1)S(1)}, u32[]{:S(2)}, u32[]{:S(2)}) collective-permute-start(bf16[2,128,512]{2,1,0:T(8,128)(2,1)S(1)} %get-tuple-element.35), channel_id=1, source_target_pairs={{0,4},{1,5},{2,6},{3,7},{4,0},{5,1},{6,2},{7,3},{8,12},{9,13},{10,... | collective-permute-start | bytes 786440 | tf_op jit(solution)/shard_map/ppermute | solution.py:12
  34.4 13.3 %collective-permute-start.3 = (bf16[2,128,512]{2,1,0:T(8,128)(2,1)S(1)}, bf16[2,128,512]{2,1,0:T(8,128)(2,1)S(1)}, u32[]{:S(2)}, u32[]{:S(2)}) collective-permute-start(bf16[2,128,512]{2,1,0:T(8,128)(2,1)S(1)} %get-tuple-element.36), channel_id=1, source_target_pairs={{0,2},{1,3},{2,0},{3,1},{4,6},{5,7},{6,4},{7,5},{8,10},{9,11},{10,... | collective-permute-start | bytes 786440 | tf_op jit(solution)/shard_map/ppermute | solution.py:12
  34.5 13.7 %collective-permute-start.1 = (bf16[2,128,512]{2,1,0:T(8,128)(2,1)S(1)}, bf16[2,128,512]{2,1,0:T(8,128)(2,1)S(1)}, u32[]{:S(2)}, u32[]{:S(2)}) collective-permute-start(bf16[2,128,512]{2,1,0:T(8,128)(2,1)S(1)} %get-tuple-element.37), channel_id=1, source_target_pairs={{0,1},{1,0},{2,3},{3,2},{4,5},{5,4},{6,7},{7,6},{8,9},{9,8},{10,11... | collective-permute-start | bytes 786440 | tf_op jit(solution)/shard_map/ppermute | solution.py:12
  64.2 7.1 %copy-start.9 = (bf16[512,512]{0,1:T(8,128)(2,1)S(1)}, bf16[512,512]{0,1:T(8,128)(2,1)}, u32[]{:S(2)}) copy-start(bf16[512,512]{0,1:T(8,128)(2,1)} %convolution_convert_fusion.3) | copy-start | bytes 1572868
  71.2 2.9 copy-start.8
  85.2 3.5 %copy-start.11 = (bf16[512,512]{0,1:T(8,128)(2,1)S(1)}, bf16[512,512]{0,1:T(8,128)(2,1)}, u32[]{:S(2)}) copy-start(bf16[512,512]{0,1:T(8,128)(2,1)} %get-tuple-element.33) | copy-start | bytes 1572868
  117.7 2.9 copy-start.7
  124.1 11.0 %copy-start.10 = (bf16[512,512]{0,1:T(8,128)(2,1)S(1)}, bf16[512,512]{0,1:T(8,128)(2,1)}, u32[]{:S(2)}) copy-start(bf16[512,512]{0,1:T(8,128)(2,1)} %get-tuple-element.32) | copy-start | bytes 1572868
  131.7 3.3 copy-start.1
  144.0 10.4 %copy-start.2 = (f32[1,1024,512]{2,1,0:T(8,128)S(1)}, f32[1,1024,512]{2,1,0:T(8,128)}, u32[]{:S(2)}) copy-start(f32[1,1024,512]{2,1,0:T(8,128)} %copy.28) | copy-start | bytes 6291460
  144.0 10.4 %copy-start.3 = (f32[1,1024,512]{2,1,0:T(8,128)S(1)}, f32[1,1024,512]{2,1,0:T(8,128)}, u32[]{:S(2)}) copy-start(f32[1,1024,512]{2,1,0:T(8,128)} %copy.29) | copy-start | bytes 6291460
  144.1 10.4 %copy-start.4 = (f32[1,1024,512]{2,1,0:T(8,128)S(1)}, f32[1,1024,512]{2,1,0:T(8,128)}, u32[]{:S(2)}) copy-start(f32[1,1024,512]{2,1,0:T(8,128)} %copy.26) | copy-start | bytes 6291460
  144.1 10.4 %copy-start.5 = (f32[1,1024,512]{2,1,0:T(8,128)S(1)}, f32[1,1024,512]{2,1,0:T(8,128)}, u32[]{:S(2)}) copy-start(f32[1,1024,512]{2,1,0:T(8,128)} %copy.27) | copy-start | bytes 6291460
  146.9 14.1 %collective-permute-start.8 = (f32[2,128,1024]{2,1,0:T(8,128)S(1)}, f32[2,128,1024]{2,1,0:T(8,128)}, u32[]{:S(2)}, u32[]{:S(2)}) collective-permute-start(f32[2,128,1024]{2,1,0:T(8,128)S(1)} %get-tuple-element.25), channel_id=1, source_target_pairs={{0,1},{1,0},{2,3},{3,2},{4,5},{5,4},{6,7},{7,6},{8,9},{9,8},{10,11... | collective-permute-start | bytes 3145736 | tf_op jit(solution)/shard_map/ppermute | solution.py:12
  153.8 44.4 %collective-permute-start.10 = (f32[2,128,1024]{2,1,0:T(8,128)S(1)}, f32[2,128,1024]{2,1,0:T(8,128)S(1)}, u32[]{:S(2)}, u32[]{:S(2)}) collective-permute-start(f32[2,128,1024]{2,1,0:T(8,128)S(1)} %get-tuple-element.23), channel_id=1, source_target_pairs={{0,4},{1,5},{2,6},{3,7},{4,0},{5,1},{6,2},{7,3},{8,12},{9,13},{10,... | collective-permute-start | bytes 3145736 | tf_op jit(solution)/shard_map/ppermute | solution.py:12
  153.9 24.8 %collective-permute-start.9 = (f32[2,128,1024]{2,1,0:T(8,128)S(1)}, f32[2,128,1024]{2,1,0:T(8,128)S(1)}, u32[]{:S(2)}, u32[]{:S(2)}) collective-permute-start(f32[2,128,1024]{2,1,0:T(8,128)S(1)} %get-tuple-element.24), channel_id=1, source_target_pairs={{0,2},{1,3},{2,0},{3,1},{4,6},{5,7},{6,4},{7,5},{8,10},{9,11},{10,... | collective-permute-start | bytes 3145736 | tf_op jit(solution)/shard_map/ppermute | solution.py:12
  155.4 2.2 copy-start.17
  155.4 2.2 copy-start.18
  155.4 2.2 copy-start.19
  155.4 3.9 %copy-start.14 = (bf16[8,64,512]{2,1,0:T(8,128)(2,1)S(1)}, bf16[8,64,512]{2,1,0:T(8,128)(2,1)}, u32[]{:S(2)}) copy-start(bf16[8,64,512]{2,1,0:T(8,128)(2,1)} %convolution_convert_fusion.2) | copy-start | bytes 1572868
  155.4 3.9 %copy-start.16 = (bf16[2,512,512]{2,1,0:T(8,128)(2,1)S(1)}, bf16[2,512,512]{2,1,0:T(8,128)(2,1)}, u32[]{:S(2)}) copy-start(bf16[2,512,512]{2,1,0:T(8,128)(2,1)} %param.8) | copy-start | bytes 3145732
  155.7 48.0 %collective-permute-start.11 = (f32[2,128,1024]{2,1,0:T(8,128)S(1)}, f32[2,128,1024]{2,1,0:T(8,128)S(1)}, u32[]{:S(2)}, u32[]{:S(2)}) collective-permute-start(f32[2,128,1024]{2,1,0:T(8,128)S(1)} %get-tuple-element.22), channel_id=1, source_target_pairs={{0,8},{1,9},{2,10},{3,11},{4,12},{5,13},{6,14},{7,15},{8,0},{9,1},... | collective-permute-start | bytes 3145736 | tf_op jit(solution)/shard_map/ppermute | solution.py:12
  204.3 1.3 copy-start.12
  210.9 6.2 %copy-start.13 = (bf16[2,512,1024]{2,1,0:T(8,128)(2,1)S(1)}, bf16[2,512,1024]{2,1,0:T(8,128)(2,1)}, u32[]{:S(2)}) copy-start(bf16[2,512,1024]{2,1,0:T(8,128)(2,1)} %copy-done.12) | copy-start | bytes 6291460
Sparse Core Ops, SparseCore 0:
  208.5 110.4 all-reduce.3
where the time goes:
time: 341 us; the launch traced here: 336 us
  waiting for transfers between devices  153 us (45%)
  matrix products  84.7 us (25%)
  local copies, waits for them, and re-layouts  48.6 us (14%)
  other arithmetic  22.2 us (7%)
  between operations  17 us (5%)
  starting transfers between devices  10.7 us (3%)
    psum x1, waiting for transfers between devices, per_device(): lax.psum((grad_query, grad_pair[:, :model_width], grad_pair[:, model_widt...  99.6 us
    ppermute x12, waiting for transfers between devices, partner(): lax.ppermute(x, axis, [(i, i ^ 1 << stride) for i in range(lax.axis_size(...  53.2 us
    sub x2, matrix products, attend(): expo_terms = jnp.exp(scores - row_max)  18.7 us
    unnamed x49, local copies, waits for them, and re-layouts  17.2 us
    dot_general x2, matrix products, attend(): jnp.einsum('sqhd,skhd->shqk', grad_context, value_heads, preferred_elemen...  15.3 us
    convert_element_type x2, other arithmetic, attend(): prob_half = probability.astype(jnp.bfloat16)  14 us
    ppermute x12, starting transfers between devices, partner(): lax.ppermute(x, axis, [(i, i ^ 1 << stride) for i in range(lax.axis_size(...  10.7 us
    dot_general x2, matrix products, attend(): jnp.einsum('shqk,skhd->sqhd', grad_score, key_heads, preferred_element_ty...  10.3 us
  transfers between devices with their start and end apart: 13, of which 6 were waited for; matrix products, arithmetic and copies ran while one was open for 12% of the time, Pallas kernels for 0%

commit v1 on v0

v1 whole, which is shorter than its diff:
```python
import functools
import math

import jax
import jax.numpy as jnp
from jax import lax
from jax.experimental import pallas as pl
from jax.experimental.pallas import tpu as pltpu
from jax.sharding import PartitionSpec as P

SUB = 128
SECTIONS = 4
LANES = 128
F32 = jnp.float32
BF16 = jnp.bfloat16


def partner(x, axis, stride):
    return lax.ppermute(x, axis, [(i, i ^ 1 << stride) for i in range(lax.axis_size(axis))])


def nt(a, b):
    return lax.dot_general(a, b, (((1,), (1,)), ((), ())), preferred_element_type=F32)


def mm(a, b):
    return jnp.dot(a, b, preferred_element_type=F32)


def attend_kernel(
    group, head_width, scale,
    mask_ref, tok_ref, arr_ref, cot_ref, wq_ref, wk_ref, wv_ref, wo_ref,
    ctx_ref, dq_ref, own_ref, part_ref, gw_ref, go_ref,
    x_ref, gq_acc, gk_acc, gv_acc, go_acc,
):
    sample = pl.program_id(0)
    rows = tok_ref.shape[1]
    keys = x_ref.shape[0]
    x_ref[:rows, :] = tok_ref[0]
    for s in range(SECTIONS):
        x_ref[rows + s * SUB : rows + (s + 1) * SUB, :] = arr_ref[s, 0]
    tok = tok_ref[0]
    x = x_ref[...]
    cot = cot_ref[0]
    q = (mm(tok, wq_ref[...]).astype(BF16).astype(F32) * scale).astype(BF16)
    k = mm(x, wk_ref[...]).astype(BF16)
    v = mm(x, wv_ref[...]).astype(BF16)
    gc = nt(cot, wo_ref[...]).astype(BF16)
    k_t, v_t, gc_t = k.T, v.T, gc.T
    lane = lax.broadcasted_iota(jnp.int32, (rows, LANES), 1)
    heads = LANES // head_width
    dk = dv = None
    ctx_t, dq_t = [], []
    for h in range(heads):
        here = (lane >= h * head_width) & (lane < (h + 1) * head_width)
        qh = jnp.where(here, q, jnp.zeros_like(q))
        gh = jnp.where(here, gc, jnp.zeros_like(gc))
        span = slice(h * head_width, (h + 1) * head_width)
        scores = nt(k, qh)
        parts = [scores[:rows]]
        for s in range(SECTIONS):
            piece = scores[rows + s * SUB : rows + (s + 1) * SUB]
            on = mask_ref[0, s, group * heads + h] > 0
            parts.append(jnp.where(on, piece, -jnp.inf))
        scores = jnp.concatenate(parts, 0)
        top = jnp.max(scores, axis=0, keepdims=True)
        expo = jnp.exp(scores - top)
        prob = expo * (1.0 / jnp.sum(expo, axis=0, keepdims=True))
        half = prob.astype(BF16)
        c_t = mm(v_t[span], half).astype(BF16)
        grad_prob = nt(v, gh)
        row_dot = jnp.sum(gc_t[span].astype(F32) * c_t.astype(F32), axis=0, keepdims=True)
        ds = (prob * (grad_prob - row_dot)).astype(BF16)
        dq_t.append((mm(k_t[span], ds) * scale).astype(BF16))
        ctx_t.append(c_t)
        dk_h, dv_h = mm(ds, qh), mm(half, gh)
        dk = dk_h if dk is None else dk + dk_h
        dv = dv_h if dv is None else dv + dv_h
    ctx_t = jnp.concatenate(ctx_t, 0)
    dq_t = jnp.concatenate(dq_t, 0)
    ctx_ref[0] = ctx_t.T
    dq_ref[0] = dq_t.T
    own_ref[0, :, :LANES] = dk[:rows]
    own_ref[0, :, LANES:] = dv[:rows]
    dkb, dvb = dk.astype(BF16), dv.astype(BF16)
    for s in range(SECTIONS):
        at = slice(rows + s * SUB, rows + (s + 1) * SUB)
        part_ref[s, 0, :, :LANES] = dkb[at]
        part_ref[s, 0, :, LANES:] = dvb[at]
    terms = (
        (gq_acc, mm(dq_t, tok)),
        (gk_acc, mm(dkb.T, x)),
        (gv_acc, mm(dvb.T, x)),
        (go_acc, mm(ctx_t, cot)),
    )

    @pl.when(sample == 0)
    def _():
        for acc, term in terms:
            acc[...] = term

    @pl.when(sample > 0)
    def _():
        for acc, term in terms:
            acc[...] += term

    @pl.when(sample == pl.num_programs(0) - 1)
    def _():
        for i, acc in enumerate((gq_acc, gk_acc, gv_acc)):
            gw_ref[:, i * LANES : (i + 1) * LANES] = acc[...].T.astype(BF16)
        go_ref[...] = go_acc[...].astype(BF16)


def attend(group, head_width, masks, tokens, arrived, cotangent, w_query, w_key, w_value, w_out):
    samples, rows, width = tokens.shape
    keys = rows + SECTIONS * SUB
    scale = 1.0 / math.sqrt(head_width)
    columns = pl.BlockSpec((width, LANES), lambda i: (0, group))
    flops = samples * (12 * rows * keys * LANES * 2 + 14 * rows * width * LANES)
    return pl.pallas_call(
        functools.partial(attend_kernel, group, head_width, scale),
        grid=(samples,),
        in_specs=[
            pl.BlockSpec(memory_space=pltpu.SMEM),
            pl.BlockSpec((1, rows, width), lambda i: (i, 0, 0)),
            pl.BlockSpec((SECTIONS, 1, SUB, width), lambda i: (0, i, 0, 0)),
            pl.BlockSpec((1, rows, width), lambda i: (i, 0, 0)),
            columns,
            columns,
            columns,
            pl.BlockSpec((LANES, width), lambda i: (group, 0)),
        ],
        out_specs=[
            pl.BlockSpec((1, rows, LANES), lambda i: (i, 0, 0)),
            pl.BlockSpec((1, rows, LANES), lambda i: (i, 0, 0)),
            pl.BlockSpec((1, rows, 2 * LANES), lambda i: (i, 0, 0)),
            pl.BlockSpec((SECTIONS, 1, SUB, 2 * LANES), lambda i: (0, i, 0, 0)),
            pl.BlockSpec((width, 3 * LANES), lambda i: (0, 0)),
            pl.BlockSpec((LANES, width), lambda i: (0, 0)),
        ],
        out_shape=[
            jax.ShapeDtypeStruct((samples, rows, LANES), BF16),
            jax.ShapeDtypeStruct((samples, rows, LANES), BF16),
            jax.ShapeDtypeStruct((samples, rows, 2 * LANES), F32),
            jax.ShapeDtypeStruct((SECTIONS, samples, SUB, 2 * LANES), BF16),
            jax.ShapeDtypeStruct((width, 3 * LANES), BF16),
            jax.ShapeDtypeStruct((LANES, width), BF16),
        ],
        scratch_shapes=[pltpu.VMEM((keys, width), BF16)]
        + [pltpu.VMEM((LANES, width), F32)] * 4,
        cost_estimate=pl.CostEstimate(
            flops=flops, bytes_accessed=8 << 20, transcendentals=samples * rows * keys * 2
        ),
        compiler_params=pltpu.CompilerParams(vmem_limit_bytes=48 << 20),
        name="attend",
    )(masks, tokens, arrived, cotangent, w_query, w_key, w_value, w_out)


def per_device(tokens, w_query, w_key, w_value, w_out, partner_block, head_masks, cotangent):
    samples, rows, width = tokens.shape
    levels = lax.axis_size("tok").bit_length() - 1
    head_width = width // head_masks.shape[2]
    sent_starts, arrived = [], []
    for s in range(SECTIONS):
        theirs = partner(partner_block, "tok", levels - 4 + s)
        sent_starts.append(theirs[0, s] * SUB)
    for s in reversed(range(SECTIONS)):
        chosen = lax.dynamic_slice_in_dim(tokens, sent_starts[s], SUB, 1)
        arrived.append(partner(chosen, "tok", levels - 4 + s))
    arrived = jnp.stack(arrived[::-1], 0)
    contexts, grad_qs, key_grads, summed = [], [], [], []
    for group in range(width // LANES):
        ctx, dq, own, part, gw, go = attend(
            group, head_width, head_masks, tokens, arrived, cotangent, w_query, w_key, w_value, w_out
        )
        contexts.append(ctx)
        grad_qs.append(dq)
        if summed:
            gw, go, _ = lax.optimization_barrier((gw, go, summed[-1]))
        summed.append(lax.psum((gw, go), "tok"))
        for s in reversed(range(SECTIONS)):
            returned = partner(part[s], "tok", levels - 4 + s).astype(F32)
            current = lax.dynamic_slice_in_dim(own, sent_starts[s], SUB, 1)
            own = lax.dynamic_update_slice_in_dim(own, current + returned, sent_starts[s], 1)
        key_grads.append(own.astype(BF16))
    flat = lambda items: jnp.concatenate(items, -1).reshape(samples * rows, -1)
    output = mm(flat(contexts), w_out).astype(BF16).reshape(samples, rows, width)
    grad_kv = key_grads
    dk = flat([g[..., :LANES] for g in grad_kv])
    dv = flat([g[..., LANES:] for g in grad_kv])
    grad_tokens = (nt(flat(grad_qs), w_query) + nt(dk, w_key) + nt(dv, w_value)).astype(BF16)
    weights = [
        jnp.concatenate([s[0][:, i * LANES : (i + 1) * LANES] for s in summed], 1).astype(F32)
        for i in range(3)
    ]
    grad_out = jnp.concatenate([s[1] for s in summed], 0).astype(F32)
    return (output, grad_tokens.reshape(samples, rows, width), *weights, grad_out)


def solution(mesh):
    placed = (
        P("groups", "tok", None),
        P(),
        P(),
        P(),
        P(),
        P("tok", None),
        P("tok", None, None),
        P("groups", "tok", None),
    )
    return jax.shard_map(
        per_device,
        mesh=mesh,
        in_specs=placed,
        out_specs=(
            P("groups", "tok", None),
            P("groups", "tok", None),
            P("groups", None),
            P("groups", None),
            P("groups", None),
            P("groups", None),
        ),
        check_vma=False,
    )
```

time: 341 us -> 492 us (1.44)
  waiting for transfers between devices: 153 us -> 362 us
  matrix products: 84.7 us -> 10.9 us
  Pallas kernels: 0 us -> 52.8 us
  local copies, waits for them, and re-layouts: 48.6 us -> 10.5 us
  starting transfers between devices: 10.7 us -> 25.8 us
  other arithmetic: 22.2 us -> 13.2 us
    psum x1 -> x4, waiting for transfers between devices: 99.6 us -> 330 us  [per_device(): summed.append(lax.psum((gw, go), 'tok'))]
    dot_general x25 -> x4, matrix products: 66 us -> 10.9 us  [the longest x3 9.21 us: nt(): lax.dot_general(a, b, (((1,), (1,)), ((), ())), preferred_element_type=F32)]
    pallas_call x0 -> x4, Pallas kernels: none -> 52.8 us  [attend(): pl.pallas_call(functools.partial(attend_kernel, group, head_width, scale)...]
    ppermute x12 -> x24, waiting for transfers between devices: 53.2 us -> 31.4 us  [partner(): lax.ppermute(x, axis, [(i, i ^ 1 << stride) for i in range(lax.axis_size(...]
    sub x2 -> x0, matrix products: 18.7 us -> none  [attend(): expo_terms = jnp.exp(scores - row_max)]
    unnamed x49 -> x44, local copies, waits for them, and re-layouts: 17.2 us -> 1.07 us
    ppermute x12 -> x24, starting transfers between devices: 10.7 us -> 25.7 us  [partner(): lax.ppermute(x, axis, [(i, i ^ 1 << stride) for i in range(lax.axis_size(...]
    reshape x5 -> x0, local copies, waits for them, and re-layouts: 12.8 us -> none  [the longest x2 6.05 us: attend(): grad_k.reshape(samples, key_count, model_width)]
  transfers between devices with their start and end apart: 13 -> 28, of which waited for: 6 -> 9; matrix products, arithmetic and copies ran while one was open for 12% -> 5% of each run, Pallas kernels for 0% -> 0%
where the time goes in v1:
time: 492 us
  waiting for transfers between devices  362 us (74%)
  Pallas kernels  52.8 us (11%)
  starting transfers between devices  25.8 us (5%)
  between operations  16.3 us (3%)
  other arithmetic  13.2 us (3%)
  matrix products  10.9 us (2%)
  local copies, waits for them, and re-layouts  10.5 us (2%)
    psum x4, waiting for transfers between devices, per_device(): summed.append(lax.psum((gw, go), 'tok'))  330 us
    pallas_call x4, Pallas kernels, attend(): pl.pallas_call(functools.partial(attend_kernel, group, head_width, scale)...  52.8 us
    ppermute x24, waiting for transfers between devices, partner(): lax.ppermute(x, axis, [(i, i ^ 1 << stride) for i in range(lax.axis_size(...  31.4 us
    ppermute x24, starting transfers between devices, partner(): lax.ppermute(x, axis, [(i, i ^ 1 << stride) for i in range(lax.axis_size(...  25.7 us
  transfers between devices with their start and end apart: 28, of which 9 were waited for; matrix products, arithmetic and copies ran while one was open for 5% of the time, Pallas kernels for 0%

profile of v1, /device:TPU:0, one launch (start us, length us, event | category | flops | bytes accessed | tf_op | source)
XLA Modules:
  0.0 491.6 jit_solution(11498300692789032069)
XLA Ops:
  7.2 3.1 collective-permute-start.2
  10.3 2.6 collective-permute-start.6
  12.9 1.6 collective-permute-start.4
  14.4 0.6 slice.121
  15.7 0.6 slice.123
  17.0 0.6 slice.122
  18.3 1.4 constant_dynamic-slice_fusion.3
  19.7 0.1 collective-permute-start.1
  19.8 1.8 collective-permute-start.7
  21.6 1.6 collective-permute-start.5
  23.2 0.5 collective-permute-start.3
  23.7 11.3 %collective-permute-done.7 = bf16[2,128,512]{2,1,0:T(8,128)(2,1)S(1)} collective-permute-done((bf16[2,128,512]{2,1,0:T(8,128)(2,1)S(1)}, bf16[2,128,512]{2,1,0:T(8,128)(2,1)S(1)}, u32[]{:S(2)}, u32[]{:S(2)}) %collective-permute-start.7) | collective-permute-done | bytes 262176 | tf_op jit(solution)/shard_map/ppermute | solution.py:19
  35.1 1.1 pad_maximum_fusion.arr_ref
  36.2 13.2 %attend.7 = (bf16[2,512,128]{2,1,0:T(8,128)(2,1)S(1)}, bf16[2,512,128]{2,1,0:T(8,128)(2,1)S(1)}, f32[2,512,256]{2,1,0:T(8,128)S(1)}, bf16[4,2,128,256]{3,2,1,0:T...) custom-call(s32[1,4,8]{2,1,0:T(4,128)S(1)} %copy-done.10, bf16[2,512,512]{2,1,0:T(8,128)(2,1)S(1)} %copy-done.2, ...), custom_call_target="tpu_custom_call" | custom-call | flops 4160749568 | bytes 8388608 | tf_op jit(solution)/shard_map/attend/pallas_call | solution.py:120
  49.4 1.0 copy-done
  50.4 13.1 %attend.6 = (bf16[2,512,128]{2,1,0:T(8,128)(2,1)S(1)}, bf16[2,512,128]{2,1,0:T(8,128)(2,1)S(1)}, f32[2,512,256]{2,1,0:T(8,128)S(1)}, bf16[4,2,128,256]{3,2,1,0:T...) custom-call(s32[1,4,8]{2,1,0:T(4,128)S(1)} %copy-done.10, bf16[2,512,512]{2,1,0:T(8,128)(2,1)S(1)} %copy-done.2, ...), custom_call_target="tpu_custom_call" | custom-call | flops 4160749568 | bytes 8388608 | tf_op jit(solution)/shard_map/attend/pallas_call | solution.py:120
  63.5 13.3 %attend.5 = (bf16[2,512,128]{2,1,0:T(8,128)(2,1)S(1)}, bf16[2,512,128]{2,1,0:T(8,128)(2,1)S(1)}, f32[2,512,256]{2,1,0:T(8,128)S(1)}, bf16[4,2,128,256]{3,2,1,0:T...) custom-call(s32[1,4,8]{2,1,0:T(4,128)S(1)} %copy-done.10, bf16[2,512,512]{2,1,0:T(8,128)(2,1)S(1)} %copy-done.2, ...), custom_call_target="tpu_custom_call" | custom-call | flops 4160749568 | bytes 8388608 | tf_op jit(solution)/shard_map/attend/pallas_call | solution.py:120
  76.8 13.2 %attend.4 = (bf16[2,512,128]{2,1,0:T(8,128)(2,1)S(1)}, bf16[2,512,128]{2,1,0:T(8,128)(2,1)S(1)}, f32[2,512,256]{2,1,0:T(8,128)S(1)}, bf16[4,2,128,256]{3,2,1,0:T...) custom-call(s32[1,4,8]{2,1,0:T(4,128)S(1)} %copy-done.10, bf16[2,512,512]{2,1,0:T(8,128)(2,1)S(1)} %copy-done.2, ...), custom_call_target="tpu_custom_call" | custom-call | flops 4160749568 | bytes 8388608 | tf_op jit(solution)/shard_map/attend/pallas_call | solution.py:120
  90.0 0.9 slice_bitcast_fusion
  90.9 0.5 collective-permute-start.22
  91.4 0.9 collective-permute-start.21
  92.2 2.4 collective-permute-start.20
  94.6 0.8 slice_bitcast_fusion.4
  95.4 0.8 slice_bitcast_fusion.8
  96.3 0.2 pad_maximum_fusion.1
  96.5 1.7 convolution_convert_fusion
  98.2 2.0 fusion.8
  100.3 1.2 slice_bitcast_fusion.12
  101.6 0.1 collective-permute-done.20
  101.7 1.5 collective-permute-start.18
  103.2 1.7 add_dynamic-update-slice_fusion.3
  104.9 1.7 add_dynamic-update-slice_fusion.2
  106.6 2.6 collective-permute-start.16
  109.2 1.7 add_dynamic-update-slice_fusion.1
  110.9 6.0 %collective-permute-done.16 = bf16[2,128,256]{2,1,0:T(8,128)(2,1)S(1)} collective-permute-done((bf16[2,128,256]{2,1,0:T(8,128)(2,1)S(1)}, bf16[2,128,256]{2,1,0:T(8,128)(2,1)S(1)}, u32[]{:S(2)}, u32[]{:S(2)}) %collective-permute-start.16) | collective-permute-done | bytes 131104 | tf_op jit(solution)/shard_map/ppermute | solution.py:19
  117.0 0.4 collective-permute-start.14
  117.5 0.1 collective-permute-start.13
  117.6 2.1 collective-permute-start.12
  119.8 0.1 add_dynamic-update-slice_fusion
  119.9 0.1 fusion.3
  120.1 0.1 fusion.2
  120.2 7.8 %collective-permute-done.12 = bf16[2,128,256]{2,1,0:T(8,128)(2,1)S(1)} collective-permute-done((bf16[2,128,256]{2,1,0:T(8,128)(2,1)S(1)}, bf16[2,128,256]{2,1,0:T(8,128)(2,1)S(1)}, u32[]{:S(2)}, u32[]{:S(2)}) %collective-permute-start.12) | collective-permute-done | bytes 131104 | tf_op jit(solution)/shard_map/ppermute | solution.py:19
  128.0 1.7 collective-permute-start.10
  129.7 0.1 collective-permute-start.9
  129.9 2.3 collective-permute-start.8
  132.2 6.0 %collective-permute-done.8 = bf16[2,128,256]{2,1,0:T(8,128)(2,1)S(1)} collective-permute-done((bf16[2,128,256]{2,1,0:T(8,128)(2,1)S(1)}, bf16[2,128,256]{2,1,0:T(8,128)(2,1)S(1)}, u32[]{:S(2)}, u32[]{:S(2)}) %collective-permute-start.8) | collective-permute-done | bytes 131104 | tf_op jit(solution)/shard_map/ppermute | solution.py:19
  138.4 0.1 add_dynamic-update-slice_fusion.8
  138.5 0.1 convert_element_type.88
  138.6 0.1 fusion.1
  138.7 0.1 fusion
  138.9 1.1 pad_maximum_fusion.4
  139.9 1.1 pad_maximum_fusion.3
  141.0 53.4 %all-reduce.15.cloned.1.call-done = (bf16[512,384]{1,0:T(8,128)(2,1)}, bf16[128,512]{1,0:T(8,128)(2,1)}) async-done(((bf16[512,384]{1,0:T(8,128)(2,1)}, bf16[128,512]{1,0:T(8,128)(2,1)}), (bf16[512,384]{1,0:T(8,128)(2,1)}, bf16[128,512]{1,0:T(8,128)(2,1)})) %all-reduce.15.cloned.1.call-update) | async-done | bytes 524304 | tf_op jit(solution)/shard_map/psum | solution.py:180
  194.6 3.5 fusion.9
  198.1 91.7 %all-reduce.13.cloned.1.call-done = (bf16[512,384]{1,0:T(8,128)(2,1)}, bf16[128,512]{1,0:T(8,128)(2,1)}) async-done(((bf16[512,384]{1,0:T(8,128)(2,1)}, bf16[128,512]{1,0:T(8,128)(2,1)}), (bf16[512,384]{1,0:T(8,128)(2,1)}, bf16[128,512]{1,0:T(8,128)(2,1)})) %all-reduce.13.cloned.1.call-update) | async-done | bytes 524304 | tf_op jit(solution)/shard_map/psum | solution.py:180
  289.9 3.7 add_convert_fusion
  293.6 0.1 fusion.4
  293.6 91.4 %all-reduce.11.cloned.1.call-done = (bf16[512,384]{1,0:T(8,128)(2,1)}, bf16[128,512]{1,0:T(8,128)(2,1)}) async-done(((bf16[512,384]{1,0:T(8,128)(2,1)}, bf16[128,512]{1,0:T(8,128)(2,1)}), (bf16[512,384]{1,0:T(8,128)(2,1)}, bf16[128,512]{1,0:T(8,128)(2,1)})) %all-reduce.11.cloned.1.call-update) | async-done | bytes 524304 | tf_op jit(solution)/shard_map/psum | solution.py:180
  385.1 0.1 fusion.5
  385.2 1.1 fusion.6
  386.2 93.9 %all-reduce.9.cloned.1.call-done = (bf16[512,384]{1,0:T(8,128)(2,1)}, bf16[128,512]{1,0:T(8,128)(2,1)}) async-done(((bf16[512,384]{1,0:T(8,128)(2,1)}, bf16[128,512]{1,0:T(8,128)(2,1)}), (bf16[512,384]{1,0:T(8,128)(2,1)}, bf16[128,512]{1,0:T(8,128)(2,1)})) %all-reduce.9.cloned.1.call-update) | async-done | bytes 524304 | tf_op jit(solution)/shard_map/psum | solution.py:180
  480.2 1.1 fusion.7
  481.3 2.3 maximum_convert_fusion.2
  483.6 1.5 maximum_convert_fusion
  (88 shorter events, 1.0 us)
Async XLA Ops:
  7.2 187.3 %all-reduce.15.cloned.1.call-start = ((), (), s32[]{:S(2)}) async-start(), calls=%async_computation.3 | async-start | bytes 1048576 | tf_op jit(solution)/shard_map/psum | solution.py:180
  7.2 7.2 %collective-permute-start.2 = (s32[1,4]{1,0:T(1,128)}, s32[1,4]{1,0:T(1,128)S(1)}, u32[]{:S(2)}, u32[]{:S(2)}) collective-permute-start(s32[1,4]{1,0:T(1,128)} %param.13), channel_id=1, source_target_pairs={{0,2},{1,3},{2,0},{3,1},{4,6},{5,7},{6,4},{7,5},{8,10},{9,11},{10,... | collective-permute-start | bytes 56 | tf_op jit(solution)/shard_map/ppermute | solution.py:19
  10.3 5.4 %collective-permute-start = (s32[1,4]{1,0:T(1,128)}, s32[1,4]{1,0:T(1,128)S(1)}, u32[]{:S(2)}, u32[]{:S(2)}) collective-permute-start(s32[1,4]{1,0:T(1,128)} %param.13), channel_id=1, source_target_pairs={{0,1},{1,0},{2,3},{3,2},{4,5},{5,4},{6,7},{7,6},{8,9},{9,8},{10,11... | collective-permute-start | bytes 56 | tf_op jit(solution)/shard_map/ppermute | solution.py:19
  10.3 5.5 %collective-permute-start.6 = (s32[1,4]{1,0:T(1,128)}, s32[1,4]{1,0:T(1,128)S(1)}, u32[]{:S(2)}, u32[]{:S(2)}) collective-permute-start(s32[1,4]{1,0:T(1,128)} %param.13), channel_id=1, source_target_pairs={{0,8},{1,9},{2,10},{3,11},{4,12},{5,13},{6,14},{7,15},{8,0},{9,1},... | collective-permute-start | bytes 56 | tf_op jit(solution)/shard_map/ppermute | solution.py:19
  12.9 4.1 collective-permute-start.4
  18.2 17.9 %copy-start.2 = (bf16[2,512,512]{2,1,0:T(8,128)(2,1)S(1)}, bf16[2,512,512]{2,1,0:T(8,128)(2,1)}, u32[]{:S(2)}) copy-start(bf16[2,512,512]{2,1,0:T(8,128)(2,1)} %tok_ref.7) | copy-start | bytes 3145732
  18.3 17.9 %copy-start.3 = (bf16[512,512]{1,0:T(8,128)(2,1)S(1)}, bf16[512,512]{1,0:T(8,128)(2,1)}, u32[]{:S(2)}) copy-start(bf16[512,512]{1,0:T(8,128)(2,1)} %wq_ref.7) | copy-start | bytes 1572868
  18.3 17.9 %copy-start.4 = (bf16[512,512]{1,0:T(8,128)(2,1)S(1)}, bf16[512,512]{1,0:T(8,128)(2,1)}, u32[]{:S(2)}) copy-start(bf16[512,512]{1,0:T(8,128)(2,1)} %wk_ref.7) | copy-start | bytes 1572868
  18.3 17.9 %copy-start.7 = (bf16[512,512]{1,0:T(8,128)(2,1)S(1)}, bf16[512,512]{1,0:T(8,128)(2,1)}, u32[]{:S(2)}) copy-start(bf16[512,512]{1,0:T(8,128)(2,1)} %wv_ref.7) | copy-start | bytes 1572868
  18.3 17.9 %copy-start.9 = (bf16[512,512]{1,0:T(8,128)(2,1)S(1)}, bf16[512,512]{1,0:T(8,128)(2,1)}, u32[]{:S(2)}) copy-start(bf16[512,512]{1,0:T(8,128)(2,1)} %wo_ref.7) | copy-start | bytes 1572868
  18.3 17.9 %copy-start.10 = (s32[1,4,8]{2,1,0:T(4,128)S(1)}, s32[1,4,8]{2,1,0:T(4,128)}, u32[]{:S(2)}) copy-start(s32[1,4,8]{2,1,0:T(4,128)} %mask_ref.7) | copy-start | bytes 388
  19.7 4.0 collective-permute-start.1
  19.8 15.2 %collective-permute-start.7 = (bf16[2,128,512]{2,1,0:T(8,128)(2,1)S(1)}, bf16[2,128,512]{2,1,0:T(8,128)(2,1)S(1)}, u32[]{:S(2)}, u32[]{:S(2)}) collective-permute-start(bf16[2,128,512]{2,1,0:T(8,128)(2,1)S(1)} %get-tuple-element.75), channel_id=1, source_target_pairs={{0,8},{1,9},{2,10},{3,11},{4,12},{5,13},{6,14},{7,15},{8,0},{9,1},... | collective-permute-start | bytes 786440 | tf_op jit(solution)/shard_map/ppermute | solution.py:19
  21.6 13.4 %collective-permute-start.5 = (bf16[2,128,512]{2,1,0:T(8,128)(2,1)S(1)}, bf16[2,128,512]{2,1,0:T(8,128)(2,1)S(1)}, u32[]{:S(2)}, u32[]{:S(2)}) collective-permute-start(bf16[2,128,512]{2,1,0:T(8,128)(2,1)S(1)} %get-tuple-element.76), channel_id=1, source_target_pairs={{0,4},{1,5},{2,6},{3,7},{4,0},{5,1},{6,2},{7,3},{8,12},{9,13},{10,... | collective-permute-start | bytes 786440 | tf_op jit(solution)/shard_map/ppermute | solution.py:19
  23.2 11.9 %collective-permute-start.3 = (bf16[2,128,512]{2,1,0:T(8,128)(2,1)S(1)}, bf16[2,128,512]{2,1,0:T(8,128)(2,1)S(1)}, u32[]{:S(2)}, u32[]{:S(2)}) collective-permute-start(bf16[2,128,512]{2,1,0:T(8,128)(2,1)S(1)} %get-tuple-element.77), channel_id=1, source_target_pairs={{0,2},{1,3},{2,0},{3,1},{4,6},{5,7},{6,4},{7,5},{8,10},{9,11},{10,... | collective-permute-start | bytes 786440 | tf_op jit(solution)/shard_map/ppermute | solution.py:19
  49.4 1.0 copy-start
  90.0 6.5 %copy-start.6 = (bf16[4,2,128,256]{3,2,1,0:T(8,128)(2,1)}, bf16[4,2,128,256]{3,2,1,0:T(8,128)(2,1)S(1)}, u32[]{:S(2)}) copy-start(bf16[4,2,128,256]{3,2,1,0:T(8,128)(2,1)S(1)} %get-tuple-element.45) | copy-start | bytes 1572868
  90.9 26.7 %collective-permute-start.23 = (bf16[2,128,256]{2,1,0:T(8,128)(2,1)}, bf16[2,128,256]{2,1,0:T(8,128)(2,1)S(1)}, u32[]{:S(2)}, u32[]{:S(2)}) collective-permute-start(bf16[2,128,256]{2,1,0:T(8,128)(2,1)} %get-tuple-element.98), channel_id=1, source_target_pairs={{0,1},{1,0},{2,3},{3,2},{4,5},{5,4},{6,7},{7,6},{8,9},{9,8},{10,11... | collective-permute-start | bytes 393224 | tf_op jit(solution)/shard_map/ppermute | solution.py:19
  90.9 15.7 %collective-permute-start.22 = (bf16[2,128,256]{2,1,0:T(8,128)(2,1)}, bf16[2,128,256]{2,1,0:T(8,128)(2,1)S(1)}, u32[]{:S(2)}, u32[]{:S(2)}) collective-permute-start(bf16[2,128,256]{2,1,0:T(8,128)(2,1)} %get-tuple-element.99), channel_id=1, source_target_pairs={{0,2},{1,3},{2,0},{3,1},{4,6},{5,7},{6,4},{7,5},{8,10},{9,11},{10,... | collective-permute-start | bytes 393224 | tf_op jit(solution)/shard_map/ppermute | solution.py:19
  91.4 13.5 %collective-permute-start.21 = (bf16[2,128,256]{2,1,0:T(8,128)(2,1)}, bf16[2,128,256]{2,1,0:T(8,128)(2,1)}, u32[]{:S(2)}, u32[]{:S(2)}) collective-permute-start(bf16[2,128,256]{2,1,0:T(8,128)(2,1)} %get-tuple-element.100), channel_id=1, source_target_pairs={{0,4},{1,5},{2,6},{3,7},{4,0},{5,1},{6,2},{7,3},{8,12},{9,13},{10,... | collective-permute-start | bytes 393224 | tf_op jit(solution)/shard_map/ppermute | solution.py:19
  92.2 9.4 %collective-permute-start.20 = (bf16[2,128,256]{2,1,0:T(8,128)(2,1)}, bf16[2,128,256]{2,1,0:T(8,128)(2,1)}, u32[]{:S(2)}, u32[]{:S(2)}) collective-permute-start(bf16[2,128,256]{2,1,0:T(8,128)(2,1)} %get-tuple-element.101), channel_id=1, source_target_pairs={{0,8},{1,9},{2,10},{3,11},{4,12},{5,13},{6,14},{7,15},{8,0},{9,1},... | collective-permute-start | bytes 393224 | tf_op jit(solution)/shard_map/ppermute | solution.py:19
  95.4 24.3 %collective-permute-start.19 = (bf16[2,128,256]{2,1,0:T(8,128)(2,1)}, bf16[2,128,256]{2,1,0:T(8,128)(2,1)S(1)}, u32[]{:S(2)}, u32[]{:S(2)}) collective-permute-start(bf16[2,128,256]{2,1,0:T(8,128)(2,1)} %get-tuple-element.94), channel_id=1, source_target_pairs={{0,1},{1,0},{2,3},{3,2},{4,5},{5,4},{6,7},{7,6},{8,9},{9,8},{10,11... | collective-permute-start | bytes 393224 | tf_op jit(solution)/shard_map/ppermute | solution.py:19
  100.3 189.5 %all-reduce.13.cloned.1.call-start = ((), (), s32[]{:S(2)}) async-start(), calls=%async_computation.2 | async-start | bytes 1048576 | tf_op jit(solution)/shard_map/psum | solution.py:180
  100.3 6.3 %copy-start.21 = (bf16[2,128,256]{2,1,0:T(8,128)(2,1)S(1)}, bf16[2,128,256]{2,1,0:T(8,128)(2,1)}, u32[]{:S(2)}) copy-start(bf16[2,128,256]{2,1,0:T(8,128)(2,1)} %get-tuple-element.97) | copy-start | bytes 393220
  100.3 16.6 %copy-start.17 = (bf16[2,128,256]{2,1,0:T(8,128)(2,1)S(1)}, bf16[2,128,256]{2,1,0:T(8,128)(2,1)}, u32[]{:S(2)}) copy-start(bf16[2,128,256]{2,1,0:T(8,128)(2,1)} %get-tuple-element.90) | copy-start | bytes 393220
  100.3 16.6 %copy-start.18 = (bf16[2,128,256]{2,1,0:T(8,128)(2,1)S(1)}, bf16[2,128,256]{2,1,0:T(8,128)(2,1)}, u32[]{:S(2)}) copy-start(bf16[2,128,256]{2,1,0:T(8,128)(2,1)} %get-tuple-element.91) | copy-start | bytes 393220
  100.3 17.1 %copy-start.19 = (bf16[2,128,256]{2,1,0:T(8,128)(2,1)S(1)}, bf16[2,128,256]{2,1,0:T(8,128)(2,1)}, u32[]{:S(2)}) copy-start(bf16[2,128,256]{2,1,0:T(8,128)(2,1)} %get-tuple-element.92) | copy-start | bytes 393220
  101.5 16.1 %copy-start.20 = (bf16[2,128,256]{2,1,0:T(8,128)(2,1)S(1)}, bf16[2,128,256]{2,1,0:T(8,128)(2,1)}, u32[]{:S(2)}) copy-start(bf16[2,128,256]{2,1,0:T(8,128)(2,1)} %get-tuple-element.93) | copy-start | bytes 393220
  101.7 15.8 %collective-permute-start.18 = (bf16[2,128,256]{2,1,0:T(8,128)(2,1)}, bf16[2,128,256]{2,1,0:T(8,128)(2,1)S(1)}, u32[]{:S(2)}, u32[]{:S(2)}) collective-permute-start(bf16[2,128,256]{2,1,0:T(8,128)(2,1)} %get-tuple-element.95), channel_id=1, source_target_pairs={{0,2},{1,3},{2,0},{3,1},{4,6},{5,7},{6,4},{7,5},{8,10},{9,11},{10,... | collective-permute-start | bytes 393224 | tf_op jit(solution)/shard_map/ppermute | solution.py:19
  104.9 12.1 %collective-permute-start.17 = (bf16[2,128,256]{2,1,0:T(8,128)(2,1)}, bf16[2,128,256]{2,1,0:T(8,128)(2,1)S(1)}, u32[]{:S(2)}, u32[]{:S(2)}) collective-permute-start(bf16[2,128,256]{2,1,0:T(8,128)(2,1)} %get-tuple-element.96), channel_id=1, source_target_pairs={{0,4},{1,5},{2,6},{3,7},{4,0},{5,1},{6,2},{7,3},{8,12},{9,13},{10,... | collective-permute-start | bytes 393224 | tf_op jit(solution)/shard_map/ppermute | solution.py:19
  106.6 10.3 %collective-permute-start.16 = (bf16[2,128,256]{2,1,0:T(8,128)(2,1)S(1)}, bf16[2,128,256]{2,1,0:T(8,128)(2,1)S(1)}, u32[]{:S(2)}, u32[]{:S(2)}) collective-permute-start(bf16[2,128,256]{2,1,0:T(8,128)(2,1)S(1)} %copy-done.21), channel_id=1, source_target_pairs={{0,8},{1,9},{2,10},{3,11},{4,12},{5,13},{6,14},{7,15},{8,0},{9,1},... | collective-permute-start | bytes 393224 | tf_op jit(solution)/shard_map/ppermute | solution.py:19
  110.9 8.9 %copy-start.1 = (f32[2,512,256]{2,1,0:T(8,128)S(1)}, f32[2,512,256]{2,1,0:T(8,128)}, u32[]{:S(2)}) copy-start(f32[2,512,256]{2,1,0:T(8,128)} %add_dynamic-update-slice_fusion.1) | copy-start | bytes 3145732
  116.9 21.5 %collective-permute-start.15 = (bf16[2,128,256]{2,1,0:T(8,128)(2,1)S(1)}, bf16[2,128,256]{2,1,0:T(8,128)(2,1)S(1)}, u32[]{:S(2)}, u32[]{:S(2)}) collective-permute-start(bf16[2,128,256]{2,1,0:T(8,128)(2,1)S(1)} %copy-done.17), channel_id=1, source_target_pairs={{0,1},{1,0},{2,3},{3,2},{4,5},{5,4},{6,7},{7,6},{8,9},{9,8},{10,11... | collective-permute-start | bytes 393224 | tf_op jit(solution)/shard_map/ppermute | solution.py:19
  117.0 12.9 %collective-permute-start.14 = (bf16[2,128,256]{2,1,0:T(8,128)(2,1)S(1)}, bf16[2,128,256]{2,1,0:T(8,128)(2,1)S(1)}, u32[]{:S(2)}, u32[]{:S(2)}) collective-permute-start(bf16[2,128,256]{2,1,0:T(8,128)(2,1)S(1)} %copy-done.18), channel_id=1, source_target_pairs={{0,2},{1,3},{2,0},{3,1},{4,6},{5,7},{6,4},{7,5},{8,10},{9,11},{10,... | collective-permute-start | bytes 393224 | tf_op jit(solution)/shard_map/ppermute | solution.py:19
  117.5 12.2 %collective-permute-start.13 = (bf16[2,128,256]{2,1,0:T(8,128)(2,1)S(1)}, bf16[2,128,256]{2,1,0:T(8,128)(2,1)S(1)}, u32[]{:S(2)}, u32[]{:S(2)}) collective-permute-start(bf16[2,128,256]{2,1,0:T(8,128)(2,1)S(1)} %copy-done.19), channel_id=1, source_target_pairs={{0,4},{1,5},{2,6},{3,7},{4,0},{5,1},{6,2},{7,3},{8,12},{9,13},{10,... | collective-permute-start | bytes 393224 | tf_op jit(solution)/shard_map/ppermute | solution.py:19
  117.6 10.4 %collective-permute-start.12 = (bf16[2,128,256]{2,1,0:T(8,128)(2,1)S(1)}, bf16[2,128,256]{2,1,0:T(8,128)(2,1)S(1)}, u32[]{:S(2)}, u32[]{:S(2)}) collective-permute-start(bf16[2,128,256]{2,1,0:T(8,128)(2,1)S(1)} %copy-done.20), channel_id=1, source_target_pairs={{0,8},{1,9},{2,10},{3,11},{4,12},{5,13},{6,14},{7,15},{8,0},{9,1},... | collective-permute-start | bytes 393224 | tf_op jit(solution)/shard_map/ppermute | solution.py:19
  119.8 18.6 %collective-permute-start.11 = (bf16[2,128,256]{2,1,0:T(8,128)(2,1)S(1)}, bf16[2,128,256]{2,1,0:T(8,128)(2,1)S(1)}, u32[]{:S(2)}, u32[]{:S(2)}) collective-permute-start(bf16[2,128,256]{2,1,0:T(8,128)(2,1)S(1)} %get-tuple-element.86), channel_id=1, source_target_pairs={{0,1},{1,0},{2,3},{3,2},{4,5},{5,4},{6,7},{7,6},{8,9},{9,8},{10,11... | collective-permute-start | bytes 393224 | tf_op jit(solution)/shard_map/ppermute | solution.py:19
  128.0 10.3 %collective-permute-start.10 = (bf16[2,128,256]{2,1,0:T(8,128)(2,1)S(1)}, bf16[2,128,256]{2,1,0:T(8,128)(2,1)S(1)}, u32[]{:S(2)}, u32[]{:S(2)}) collective-permute-start(bf16[2,128,256]{2,1,0:T(8,128)(2,1)S(1)} %get-tuple-element.87), channel_id=1, source_target_pairs={{0,2},{1,3},{2,0},{3,1},{4,6},{5,7},{6,4},{7,5},{8,10},{9,11},{10,... | collective-permute-start | bytes 393224 | tf_op jit(solution)/shard_map/ppermute | solution.py:19
  129.7 8.5 %collective-permute-start.9 = (bf16[2,128,256]{2,1,0:T(8,128)(2,1)S(1)}, bf16[2,128,256]{2,1,0:T(8,128)(2,1)S(1)}, u32[]{:S(2)}, u32[]{:S(2)}) collective-permute-start(bf16[2,128,256]{2,1,0:T(8,128)(2,1)S(1)} %get-tuple-element.88), channel_id=1, source_target_pairs={{0,4},{1,5},{2,6},{3,7},{4,0},{5,1},{6,2},{7,3},{8,12},{9,13},{10,... | collective-permute-start | bytes 393224 | tf_op jit(solution)/shard_map/ppermute | solution.py:19
  129.9 8.3 %collective-permute-start.8 = (bf16[2,128,256]{2,1,0:T(8,128)(2,1)S(1)}, bf16[2,128,256]{2,1,0:T(8,128)(2,1)S(1)}, u32[]{:S(2)}, u32[]{:S(2)}) collective-permute-start(bf16[2,128,256]{2,1,0:T(8,128)(2,1)S(1)} %get-tuple-element.89), channel_id=1, source_target_pairs={{0,8},{1,9},{2,10},{3,11},{4,12},{5,13},{6,14},{7,15},{8,0},{9,1},... | collective-permute-start | bytes 393224 | tf_op jit(solution)/shard_map/ppermute | solution.py:19
  138.8 55.7 %copy-start.5 = (bf16[512,512]{1,0:T(8,128)(2,1)S(1)}, bf16[512,512]{1,0:T(8,128)(2,1)}, u32[]{:S(2)}) copy-start(bf16[512,512]{1,0:T(8,128)(2,1)} %wk_ref.7) | copy-start | bytes 1572868
  194.5 190.5 %all-reduce.11.cloned.1.call-start = ((), (), s32[]{:S(2)}) async-start(), calls=%async_computation.1 | async-start | bytes 1048576 | tf_op jit(solution)/shard_map/psum | solution.py:180
  194.6 95.3 %copy-start.8 = (bf16[512,512]{1,0:T(8,128)(2,1)S(1)}, bf16[512,512]{1,0:T(8,128)(2,1)}, u32[]{:S(2)}) copy-start(bf16[512,512]{1,0:T(8,128)(2,1)} %wv_ref.7) | copy-start | bytes 1572868
  194.6 95.3 %copy-start.11 = (f32[1024,512]{1,0:T(8,128)S(1)}, f32[1024,512]{1,0:T(8,128)}, u32[]{:S(2)}) copy-start(f32[1024,512]{1,0:T(8,128)} %fusion.8) | copy-start | bytes 6291460
  289.8 190.4 %all-reduce.9.cloned.1.call-start = ((), (), s32[]{:S(2)}) async-start(), calls=%async_computation | async-start | bytes 1048576 | tf_op jit(solution)/shard_map/psum | solution.py:180
  289.9 3.7 copy-start.12
  289.9 95.2 %copy-start.13 = (bf16[512,384]{1,0:T(8,128)(2,1)S(1)}, bf16[512,384]{1,0:T(8,128)(2,1)}, u32[]{:S(2)}) copy-start(bf16[512,384]{1,0:T(8,128)(2,1)} %get-tuple-element.70) | copy-start | bytes 1179652
  293.6 187.7 %copy-start.14 = (bf16[128,512]{1,0:T(8,128)(2,1)S(1)}, bf16[128,512]{1,0:T(8,128)(2,1)}, u32[]{:S(2)}) copy-start(bf16[128,512]{1,0:T(8,128)(2,1)} %get-tuple-element.73) | copy-start | bytes 393220
  293.6 187.7 %copy-start.15 = (bf16[128,512]{1,0:T(8,128)(2,1)S(1)}, bf16[128,512]{1,0:T(8,128)(2,1)}, u32[]{:S(2)}) copy-start(bf16[128,512]{1,0:T(8,128)(2,1)} %get-tuple-element.71) | copy-start | bytes 393220
  385.1 96.2 %copy-start.16 = (bf16[128,512]{1,0:T(8,128)(2,1)S(1)}, bf16[128,512]{1,0:T(8,128)(2,1)}, u32[]{:S(2)}) copy-start(bf16[128,512]{1,0:T(8,128)(2,1)} %get-tuple-element.69) | copy-start | bytes 393220
Sparse Core Ops, SparseCore 0:
  100.4 94.0 all-reduce.14
  198.5 91.2 all-reduce.12
  293.8 91.2 all-reduce.10
  388.9 91.1 all-reduce.8

commit v2 on v1

v2 whole, which is shorter than its diff:
```python
import functools
import math

import jax
import jax.numpy as jnp
from jax import lax
from jax.experimental import pallas as pl
from jax.experimental.pallas import tpu as pltpu
from jax.sharding import PartitionSpec as P

SUB = 128
SECTIONS = 4
LANES = 128
F32 = jnp.float32
BF16 = jnp.bfloat16
MESH = pl.DeviceIdType.MESH


def nt(a, b):
    return lax.dot_general(a, b, (((1,), (1,)), ((), ())), preferred_element_type=F32)


def mm(a, b):
    return jnp.dot(a, b, preferred_element_type=F32)


def attend_kernel(
    head_width, scale,
    mask_ref, tok_ref, arr_ref, cot_ref, wq_ref, wk_ref, wv_ref, wo_ref,
    ctx_ref, dq_ref, own_ref, part_ref, gw_ref, go_ref,
    x_ref, gq_acc, gk_acc, gv_acc, go_acc,
):
    group, sample = pl.program_id(0), pl.program_id(1)
    rows = tok_ref.shape[1]
    keys = x_ref.shape[0]
    x_ref[:rows, :] = tok_ref[0]
    for s in range(SECTIONS):
        x_ref[rows + s * SUB : rows + (s + 1) * SUB, :] = arr_ref[s, 0]
    tok = tok_ref[0]
    x = x_ref[...]
    cot = cot_ref[0]
    q = (mm(tok, wq_ref[...]).astype(BF16).astype(F32) * scale).astype(BF16)
    k = mm(x, wk_ref[...]).astype(BF16)
    v = mm(x, wv_ref[...]).astype(BF16)
    gc = nt(cot, wo_ref[...]).astype(BF16)
    k_t, v_t, gc_t = k.T, v.T, gc.T
    lane = lax.broadcasted_iota(jnp.int32, (rows, LANES), 1)
    heads = LANES // head_width
    dk = dv = None
    ctx_t, dq_t = [], []
    for h in range(heads):
        here = (lane >= h * head_width) & (lane < (h + 1) * head_width)
        qh = jnp.where(here, q, jnp.zeros_like(q))
        gh = jnp.where(here, gc, jnp.zeros_like(gc))
        span = slice(h * head_width, (h + 1) * head_width)
        scores = nt(k, qh)
        parts = [scores[:rows]]
        for s in range(SECTIONS):
            piece = scores[rows + s * SUB : rows + (s + 1) * SUB]
            on = mask_ref[0, s, group * heads + h] > 0
            parts.append(jnp.where(on, piece, -jnp.inf))
        scores = jnp.concatenate(parts, 0)
        top = jnp.max(scores, axis=0, keepdims=True)
        expo = jnp.exp(scores - top)
        prob = expo * (1.0 / jnp.sum(expo, axis=0, keepdims=True))
        half = prob.astype(BF16)
        c_t = mm(v_t[span], half).astype(BF16)
        grad_prob = nt(v, gh)
        row_dot = jnp.sum(gc_t[span].astype(F32) * c_t.astype(F32), axis=0, keepdims=True)
        ds = (prob * (grad_prob - row_dot)).astype(BF16)
        dq_t.append((mm(k_t[span], ds) * scale).astype(BF16))
        ctx_t.append(c_t)
        dk_h, dv_h = mm(ds, qh), mm(half, gh)
        dk = dk_h if dk is None else dk + dk_h
        dv = dv_h if dv is None else dv + dv_h
    ctx_t = jnp.concatenate(ctx_t, 0)
    dq_t = jnp.concatenate(dq_t, 0)
    ctx_ref[0] = ctx_t.T
    dq_ref[0] = dq_t.T
    own_ref[0, 0] = dk[:rows]
    own_ref[1, 0] = dv[:rows]
    dkb, dvb = dk.astype(BF16), dv.astype(BF16)
    for s in range(SECTIONS):
        at = slice(rows + s * SUB, rows + (s + 1) * SUB)
        part_ref[s, 0, 0] = dkb[at]
        part_ref[s, 1, 0] = dvb[at]
    terms = (
        (gq_acc, mm(dq_t, tok)),
        (gk_acc, mm(dkb.T, x)),
        (gv_acc, mm(dvb.T, x)),
        (go_acc, mm(ctx_t, cot)),
    )

    @pl.when(sample == 0)
    def _():
        for acc, term in terms:
            acc[...] = term

    @pl.when(sample > 0)
    def _():
        for acc, term in terms:
            acc[...] += term

    @pl.when(sample == pl.num_programs(1) - 1)
    def _():
        for i, acc in enumerate((gq_acc, gk_acc, gv_acc)):
            gw_ref[i] = acc[...].T.astype(BF16)
        go_ref[...] = go_acc[...].astype(BF16)


def attend(head_width, masks, tokens, arrived, cotangent, w_query, w_key, w_value, w_out):
    samples, rows, width = tokens.shape
    keys = rows + SECTIONS * SUB
    scale = 1.0 / math.sqrt(head_width)
    columns = pl.BlockSpec((width, LANES), lambda g, i: (0, g))
    whole_row = pl.BlockSpec((1, rows, width), lambda g, i: (i, 0, 0))
    row_columns = pl.BlockSpec((1, rows, LANES), lambda g, i: (i, 0, g))
    return pl.pallas_call(
        functools.partial(attend_kernel, head_width, scale),
        grid=(width // LANES, samples),
        in_specs=[
            pl.BlockSpec(memory_space=pltpu.SMEM),
            whole_row,
            pl.BlockSpec((SECTIONS, 1, SUB, width), lambda g, i: (0, i, 0, 0)),
            whole_row,
            columns,
            columns,
            columns,
            pl.BlockSpec((LANES, width), lambda g, i: (g, 0)),
        ],
        out_specs=[
            row_columns,
            row_columns,
            pl.BlockSpec((2, 1, rows, LANES), lambda g, i: (0, i, 0, g)),
            pl.BlockSpec((SECTIONS, 2, 1, SUB, LANES), lambda g, i: (0, 0, i, 0, g)),
            pl.BlockSpec((3, width, LANES), lambda g, i: (0, 0, g)),
            pl.BlockSpec((LANES, width), lambda g, i: (g, 0)),
        ],
        out_shape=[
            jax.ShapeDtypeStruct((samples, rows, width), BF16),
            jax.ShapeDtypeStruct((samples, rows, width), BF16),
            jax.ShapeDtypeStruct((2, samples, rows, width), F32),
            jax.ShapeDtypeStruct((SECTIONS, 2, samples, SUB, width), BF16),
            jax.ShapeDtypeStruct((3, width, width), BF16),
            jax.ShapeDtypeStruct((width, width), BF16),
        ],
        scratch_shapes=[pltpu.VMEM((keys, width), BF16)]
        + [pltpu.VMEM((LANES, width), F32)] * 4,
        compiler_params=pltpu.CompilerParams(vmem_limit_bytes=48 << 20),
        name="attend",
    )(masks, tokens, arrived, cotangent, w_query, w_key, w_value, w_out)


def toward(bit):
    me = lax.axis_index("tok")
    mine = (me // (1 << bit)) % 2
    return mine, {"tok": me + (1 - 2 * mine) * (1 << bit)}


def greet(bits):
    barrier = pltpu.get_barrier_semaphore()
    for bit in bits:
        pl.semaphore_signal(barrier, inc=1, device_id=toward(bit)[1], device_id_type=MESH)
    pl.semaphore_wait(barrier, len(bits))


def send(src, dst, send_sem, recv_sem, bit):
    copy = pltpu.make_async_remote_copy(
        src_ref=src, dst_ref=dst, send_sem=send_sem, recv_sem=recv_sem,
        device_id=toward(bit)[1], device_id_type=MESH,
    )
    copy.start()
    return copy


def fetch_kernel(
    levels, choice_ref, tok_ref, arrived_ref, theirs_ref,
    chosen, landed, wanted, choice_send, choice_recv, tok_send, tok_recv,
):
    samples, rows, width = tok_ref.shape
    first = levels - SECTIONS
    greet([first + s for s in range(SECTIONS)])
    asks = [
        send(choice_ref.at[s], wanted.at[s], choice_send.at[s], choice_recv.at[s], first + s)
        for s in range(SECTIONS)
    ]
    copies = []
    for s in reversed(range(SECTIONS)):
        asks[s].wait()
        pick = jnp.broadcast_to(wanted[s, 0:1, 0:1], (SUB, width))
        for i in range(samples):
            value = tok_ref[i, :SUB, :].astype(F32)
            for block in range(1, rows // SUB):
                other = tok_ref[i, block * SUB : (block + 1) * SUB, :].astype(F32)
                value = jnp.where(pick == block, other, value)
            chosen[s, i] = value.astype(BF16)
        copies.append(
            (s, send(chosen.at[s], landed.at[s], tok_send.at[s], tok_recv.at[s], first + s))
        )
    theirs_ref[...] = wanted[...]
    for s, copy in reversed(copies):
        copy.wait()
        arrived_ref[s] = landed[s]


def fetch(levels, choice, tokens):
    samples, rows, width = tokens.shape
    vmem = pl.BlockSpec(memory_space=pltpu.VMEM)
    size = (SECTIONS, samples, SUB, width)
    sems = pltpu.SemaphoreType.DMA((SECTIONS,))
    return pl.pallas_call(
        functools.partial(fetch_kernel, levels),
        in_specs=[vmem, vmem],
        out_specs=[vmem, vmem],
        out_shape=[
            jax.ShapeDtypeStruct(size, BF16),
            jax.ShapeDtypeStruct(choice.shape, jnp.int32),
        ],
        scratch_shapes=[
            pltpu.VMEM(size, BF16),
            pltpu.VMEM(size, BF16),
            pltpu.VMEM(choice.shape, jnp.int32),
            sems, sems, sems, sems,
        ],
        compiler_params=pltpu.CompilerParams(collective_id=0, has_side_effects=True),
        name="fetch",
    )(choice, tokens)


def settle_kernel(
    levels, part_ref, gw_ref, go_ref, ret_ref, sum_ref,
    landed, acc, got, full, part_send, part_recv, rs_send, rs_recv, ag_send, ag_recv,
):
    width = go_ref.shape[0]
    for i in range(3):
        acc[i * width : (i + 1) * width, :] = gw_ref[i]
    acc[3 * width :, :] = go_ref[...]
    greet(list(range(levels)))
    half_rows = 2 * width
    straight = list(range(levels))
    orders = (straight, [0] + straight[2:] + [1])
    base = [lane * half_rows for lane in range(2)]
    size, inbox = half_rows, [lane * half_rows for lane in range(2)]
    lanes = range(2)

    def window(ref, start, count):
        return ref.at[pl.ds(pl.multiple_of(start, count), count), :]

    def scatter(lane, step, size):
        bit, half = orders[lane][step], size // 2
        mine, _ = toward(bit)
        away = base[lane] + (1 - mine) * half
        copy = send(
            window(acc, away, half), window(got, inbox[lane], half),
            rs_send.at[lane, step], rs_recv.at[lane, step], bit,
        )
        base[lane] = base[lane] + mine * half
        return copy

    flying = [scatter(lane, 0, size) for lane in lanes]
    first = levels - SECTIONS
    returns = [
        send(part_ref.at[s], landed.at[s], part_send.at[s], part_recv.at[s], first + s)
        for s in reversed(range(SECTIONS))
    ]
    for step in range(levels):
        half = size // 2
        for lane in lanes:
            flying[lane].wait()
            here = pl.ds(pl.multiple_of(base[lane], half), half)
            total = acc[here, :].astype(F32) + got[inbox[lane] : inbox[lane] + half, :].astype(F32)
            inbox[lane] += half
            if step < levels - 1:
                acc[here, :] = total.astype(BF16)
                flying[lane] = scatter(lane, step + 1, half)
            else:
                full[here, :] = total.astype(BF16)
        size = half
    for step in reversed(range(levels)):
        for lane in lanes:
            if step < levels - 1:
                flying[lane].wait()
                base[lane] = base[lane] - toward(orders[lane][step + 1])[0] * (size // 2)
            held = window(full, base[lane], size)
            flying[lane] = send(
                held, held, ag_send.at[lane, step], ag_recv.at[lane, step], orders[lane][step]
            )
        size *= 2
    for lane in lanes:
        flying[lane].wait()
    sum_ref[...] = full[...]
    for copy in returns:
        copy.wait()
    ret_ref[...] = landed[...]


def settle(levels, part, gw, go):
    width = go.shape[0]
    vmem = pl.BlockSpec(memory_space=pltpu.VMEM)
    stack = (4 * width, width)
    four = pltpu.SemaphoreType.DMA((SECTIONS,))
    steps = pltpu.SemaphoreType.DMA((2, levels))
    return pl.pallas_call(
        functools.partial(settle_kernel, levels),
        in_specs=[vmem] * 3,
        out_specs=[vmem] * 2,
        out_shape=[
            jax.ShapeDtypeStruct(part.shape, BF16),
            jax.ShapeDtypeStruct(stack, BF16),
        ],
        scratch_shapes=[pltpu.VMEM(part.shape, BF16)]
        + [pltpu.VMEM(stack, BF16)] * 3
        + [four, four, steps, steps, steps, steps],
        compiler_params=pltpu.CompilerParams(
            collective_id=1, has_side_effects=True, vmem_limit_bytes=48 << 20
        ),
        name="settle",
    )(part, gw, go)


def finish_kernel(
    start_ref, own_ref, ret_ref, ctx_ref, dq_ref, wq_ref, wk_ref, wv_ref, wo_ref, sum_ref,
    out_ref, gtok_ref, gq_ref, gk_ref, gv_ref, go_ref, key_grads,
):
    out_ref[0] = mm(ctx_ref[0], wo_ref[...]).astype(BF16)
    key_grads[...] = own_ref[:, 0]
    for s in range(SECTIONS):
        at = pl.ds(pl.multiple_of(start_ref[s], SUB), SUB)
        key_grads[:, at, :] += ret_ref[s, :, 0].astype(F32)
    gtok_ref[0] = (
        nt(dq_ref[0], wq_ref[...])
        + nt(key_grads[0].astype(BF16), wk_ref[...])
        + nt(key_grads[1].astype(BF16), wv_ref[...])
    ).astype(BF16)
    for i, ref in enumerate((gq_ref, gk_ref, gv_ref, go_ref)):
        ref[...] = sum_ref[i].astype(F32)


def finish(starts, own, ret, ctx, dq, w_query, w_key, w_value, w_out, sums):
    samples, rows, width = ctx.shape
    row = pl.BlockSpec((1, rows, width), lambda i: (i, 0, 0))
    weight = pl.BlockSpec((width, width), lambda i: (0, 0))
    share = width // samples
    grad = pl.BlockSpec((share, width), lambda i: (i, 0))
    return pl.pallas_call(
        finish_kernel,
        grid=(samples,),
        in_specs=[
            pl.BlockSpec(memory_space=pltpu.SMEM),
            pl.BlockSpec((2, 1, rows, width), lambda i: (0, i, 0, 0)),
            pl.BlockSpec((SECTIONS, 2, 1, SUB, width), lambda i: (0, 0, i, 0, 0)),
            row, row, weight, weight, weight, weight,
            pl.BlockSpec((4, share, width), lambda i: (0, i, 0)),
        ],
        out_specs=[row, row, grad, grad, grad, grad],
        out_shape=[jax.ShapeDtypeStruct(ctx.shape, BF16)] * 2
        + [jax.ShapeDtypeStruct((width, width), F32)] * 4,
        scratch_shapes=[pltpu.VMEM((2, rows, width), F32)],
        compiler_params=pltpu.CompilerParams(vmem_limit_bytes=48 << 20),
        name="finish",
    )(starts, own, ret, ctx, dq, w_query, w_key, w_value, w_out, sums)


def per_device(tokens, w_query, w_key, w_value, w_out, partner_block, head_masks, cotangent):
    width = tokens.shape[2]
    levels = lax.axis_size("tok").bit_length() - 1
    head_width = width // head_masks.shape[2]
    choice = jnp.broadcast_to(partner_block[0][:, None, None], (SECTIONS, 8, LANES))
    arrived, theirs = fetch(levels, choice, tokens)
    ctx, dq, own, part, gw, go = attend(
        head_width, head_masks, tokens, arrived, cotangent, w_query, w_key, w_value, w_out
    )
    ret, sums = settle(levels, part, gw, go)
    starts = theirs[:, 0, 0] * SUB
    return finish(
        starts, own, ret, ctx, dq, w_query, w_key, w_value, w_out, sums.reshape(4, width, width)
    )


def solution(mesh):
    placed = (
        P("groups", "tok", None),
        P(),
        P(),
        P(),
        P(),
        P("tok", None),
        P("tok", None, None),
        P("groups", "tok", None),
    )
    return jax.shard_map(
        per_device,
        mesh=mesh,
        in_specs=placed,
        out_specs=(
            P("groups", "tok", None),
            P("groups", "tok", None),
            P("groups", None),
            P("groups", None),
            P("groups", None),
            P("groups", None),
        ),
        check_vma=False,
    )
```

time: 492 us -> 156 us (0.32)
  waiting for transfers between devices: 362 us -> 0 us
  Pallas kernels: 52.8 us -> 144 us
  starting transfers between devices: 25.8 us -> 0 us
  between operations: 16.3 us -> 0.68 us
  other arithmetic: 13.2 us -> 0.88 us
  matrix products: 10.9 us -> 0 us
    psum x4 -> x0, waiting for transfers between devices: 330 us -> none  [per_device(): summed.append(lax.psum((gw, go), 'tok'))]
    pallas_call x4, Pallas kernels: 52.8 us -> 144 us  [the longest x1 67.6 us: settle(): pl.pallas_call(functools.partial(settle_kernel, levels), in_specs=[vmem]...]
    ppermute x24 -> x0, waiting for transfers between devices: 31.4 us -> none  [partner(): lax.ppermute(x, axis, [(i, i ^ 1 << stride) for i in range(lax.axis_size(...]
    ppermute x24 -> x0, starting transfers between devices: 25.7 us -> none  [partner(): lax.ppermute(x, axis, [(i, i ^ 1 << stride) for i in range(lax.axis_size(...]
    dot_general x4 -> x0, matrix products: 10.9 us -> none  [the longest x3 9.21 us: nt(): lax.dot_general(a, b, (((1,), (1,)), ((), ())), preferred_element_type=F32)]
    unnamed x44 -> x24, local copies, waits for them, and re-layouts: 1.07 us -> 8.81 us
    dynamic_update_slice x14 -> x0, other arithmetic: 5.67 us -> none  [per_device(): lax.dynamic_update_slice_in_dim(own, current + returned, sent_starts[s], 1)]
  transfers between devices with their start and end apart: 28 -> 0, of which waited for: 9 -> 0; matrix products, arithmetic and copies ran while one was open for 5% -> 0% of each run, Pallas kernels for 0% -> 0%
where the time goes in v2:
time: 156 us
  Pallas kernels  144 us (92%)
  local copies, waits for them, and re-layouts  10.1 us (6%)
    pallas_call x1, Pallas kernels, settle(): pl.pallas_call(functools.partial(settle_kernel, levels), in_specs=[vmem]...  67.6 us
    pallas_call x1, Pallas kernels, attend(): pl.pallas_call(functools.partial(attend_kernel, head_width, scale), grid=...  47.7 us
    pallas_call x1, Pallas kernels, fetch(): pl.pallas_call(functools.partial(fetch_kernel, levels), in_specs=[vmem, v...  22 us
    unnamed x24, local copies, waits for them, and re-layouts  8.81 us
    pallas_call x1, Pallas kernels, finish(): pl.pallas_call(finish_kernel, grid=(samples,), in_specs=[pl.BlockSpec(mem...  6.9 us

profile of v2, /device:TPU:0, one launch (start us, length us, event | category | flops | bytes accessed | tf_op | source)
XLA Modules:
  0.0 155.9 jit_solution(5899226918625864745)
XLA Ops:
  0.6 1.3 broadcast_in_dim.8.choice_ref
  2.0 22.0 %fetch.1 = (bf16[4,2,128,512]{3,2,1,0:T(8,128)(2,1)}, s32[4,8,128]{2,1,0:T(8,128)}) custom-call(s32[4,8,128]{2,1,0:T(8,128)} %broadcast_in_dim.8.choice_ref, bf16[2,512,512]{2,1,0:T(8,128)(2,1)} %tok_ref.3), custom_call_target="tpu_custom_call" | custom-call | tf_op jit(solution)/shard_map/fetch/pallas_call | solution.py:211
  24.0 0.9 multiply_reduce_fusion.start_ref
  24.9 0.0 copy-start
  24.9 1.2 copy-done
  26.1 0.0 copy-start.2
  26.1 1.0 copy-done.2
  27.2 0.0 copy-start.4
  27.2 1.0 copy-done.4
  28.2 0.0 copy-start.6
  28.2 1.0 copy-done.6
  29.2 0.0 copy-start.8
  29.2 1.0 copy-done.8
  30.3 0.0 copy-start.11
  30.3 0.7 copy-done.11
  31.0 47.7 %attend.1 = (bf16[2,512,512]{2,1,0:T(8,128)(2,1)S(1)}, bf16[2,512,512]{2,1,0:T(8,128)(2,1)S(1)}, f32[2,2,512,512]{3,2,1,0:T(8,128)}, bf16[4,2,2,128,512]{4,3,2,1...) custom-call(s32[1,4,8]{2,1,0:T(4,128)S(1)} %copy-done.11, bf16[2,512,512]{2,1,0:T(8,128)(2,1)S(1)} %copy-done, ...), custom_call_target="tpu_custom_call" | custom-call | tf_op jit(solution)/shard_map/attend/pallas_call | solution.py:118
  78.7 0.0 copy-start.10
  78.7 1.4 copy-done.10
  80.1 0.0 copy-start.3
  80.1 0.0 copy-start.5
  80.1 0.0 copy-start.7
  80.1 0.0 copy-start.9
  80.1 67.6 %settle.1 = (bf16[4,2,2,128,512]{4,3,2,1,0:T(8,128)(2,1)S(1)}, bf16[2048,512]{1,0:T(8,128)(2,1)}) custom-call(bf16[4,2,2,128,512]{4,3,2,1,0:T(8,128)(2,1)} %get-tuple-element.19.part_ref, bf16[3,512,512]{2,1,0:T(8,128)(2,1)S(1)} %copy-done.10, bf16[512,512]{1,0:T(8,128)(2,1)S(1)} %get-tuple-element.21.go_ref), custom_call_target="tpu_custom_call" | custom-call | tf_op jit(solution)/shard_map/settle/pallas_call | solution.py:303
  147.7 0.0 copy-start.1
  147.7 1.3 copy-done.1
  149.0 0.0 copy-done.3
  149.0 0.0 copy-done.5
  149.0 0.0 copy-done.7
  149.0 0.0 copy-done.9
  149.0 6.9 %finish.1 = (bf16[2,512,512]{2,1,0:T(8,128)(2,1)}, bf16[2,512,512]{2,1,0:T(8,128)(2,1)}, f32[512,512]{1,0:T(8,128)}, f32[512,512]{1,0:T(8,128)}, f32[512,512]{1,0:T(8,128)}, /*index=5*/f32[512,512]{1,0:T(8,128)}) custom-call(s32[4]{0:T(128)S(1)} %multiply_reduce_fusion.start_ref, f32[2,2,512,512]{3,2,1,0:T(8,128)} %get-tuple-element.18.own_ref, ...), custom_call_target="tpu_custom_call" | custom-call | tf_op jit(solution)/shard_map/finish/pallas_call | solution.py:345
Async XLA Ops:
  24.9 1.2 copy-start
  26.1 1.0 copy-start.2
  27.2 1.0 copy-start.4
  28.2 1.0 copy-start.6
  29.2 1.0 copy-start.8
  30.3 0.7 copy-start.11
  78.7 1.4 copy-start.10
  80.1 68.9 %copy-start.3 = (bf16[512,512]{1,0:T(8,128)(2,1)S(1)}, bf16[512,512]{1,0:T(8,128)(2,1)}, u32[]{:S(2)}) copy-start(bf16[512,512]{1,0:T(8,128)(2,1)} %wq_ref.3) | copy-start | bytes 1572868
  80.1 68.9 %copy-start.5 = (bf16[512,512]{1,0:T(8,128)(2,1)S(1)}, bf16[512,512]{1,0:T(8,128)(2,1)}, u32[]{:S(2)}) copy-start(bf16[512,512]{1,0:T(8,128)(2,1)} %wk_ref.3) | copy-start | bytes 1572868
  80.1 68.9 %copy-start.7 = (bf16[512,512]{1,0:T(8,128)(2,1)S(1)}, bf16[512,512]{1,0:T(8,128)(2,1)}, u32[]{:S(2)}) copy-start(bf16[512,512]{1,0:T(8,128)(2,1)} %wv_ref.3) | copy-start | bytes 1572868
  80.1 68.9 %copy-start.9 = (bf16[512,512]{1,0:T(8,128)(2,1)S(1)}, bf16[512,512]{1,0:T(8,128)(2,1)}, u32[]{:S(2)}) copy-start(bf16[512,512]{1,0:T(8,128)(2,1)} %wo_ref.3) | copy-start | bytes 1572868
  147.7 1.3 copy-start.1

commit v3 on v2

--- a/solution.py
+++ b/solution.py
@@ -8,14 +8,20 @@
 from jax.experimental.pallas import tpu as pltpu
 from jax.sharding import PartitionSpec as P
 
+
 SUB = 128
 SECTIONS = 4
 LANES = 128
+LATE = 1
 F32 = jnp.float32
 BF16 = jnp.bfloat16
 MESH = pl.DeviceIdType.MESH
 
 
+def partner(x, axis, stride):
+    return lax.ppermute(x, axis, [(i, i ^ 1 << stride) for i in range(lax.axis_size(axis))])
+
+
 def nt(a, b):
     return lax.dot_general(a, b, (((1,), (1,)), ((), ())), preferred_element_type=F32)
 
@@ -25,14 +31,13 @@
 
 
 def attend_kernel(
-    head_width, scale,
-    mask_ref, tok_ref, arr_ref, cot_ref, wq_ref, wk_ref, wv_ref, wo_ref,
-    ctx_ref, dq_ref, own_ref, part_ref, gw_ref, go_ref,
-    x_ref, gq_acc, gk_acc, gv_acc, go_acc,
+    head_width, scale, first, held,
+    mask_ref, tok_ref, arr_ref, cot_ref, wq_ref, wk_ref, wv_ref, wo_ref, *refs,
 ):
-    group, sample = pl.program_id(0), pl.program_id(1)
+    ctx_ref, dq_ref, own_ref, gw_ref, go_ref, part_ref = refs[held : held + 6]
+    x_ref, gq_acc, gk_acc, gv_acc, go_acc = refs[held + 6 :]
+    group, sample = first + pl.program_id(0), pl.program_id(1)
     rows = tok_ref.shape[1]
-    keys = x_ref.shape[0]
     x_ref[:rows, :] = tok_ref[0]
     for s in range(SECTIONS):
         x_ref[rows + s * SUB : rows + (s + 1) * SUB, :] = arr_ref[s, 0]
@@ -108,16 +113,19 @@
         go_ref[...] = go_acc[...].astype(BF16)
 
 
-def attend(head_width, masks, tokens, arrived, cotangent, w_query, w_key, w_value, w_out):
+def attend(
+    head_width, first, count, held,
+    masks, tokens, arrived, cotangent, w_query, w_key, w_value, w_out,
+):
     samples, rows, width = tokens.shape
     keys = rows + SECTIONS * SUB
     scale = 1.0 / math.sqrt(head_width)
-    columns = pl.BlockSpec((width, LANES), lambda g, i: (0, g))
+    columns = pl.BlockSpec((width, LANES), lambda g, i: (0, first + g))
     whole_row = pl.BlockSpec((1, rows, width), lambda g, i: (i, 0, 0))
-    row_columns = pl.BlockSpec((1, rows, LANES), lambda g, i: (i, 0, g))
+    row_columns = pl.BlockSpec((1, rows, LANES), lambda g, i: (i, 0, first + g))
     return pl.pallas_call(
-        functools.partial(attend_kernel, head_width, scale),
-        grid=(width // LANES, samples),
+        functools.partial(attend_kernel, head_width, scale, first, len(held)),
+        grid=(count, samples),
         in_specs=[
             pl.BlockSpec(memory_space=pltpu.SMEM),
             whole_row,
@@ -126,29 +134,35 @@
             columns,
             columns,
             columns,
-            pl.BlockSpec((LANES, width), lambda g, i: (g, 0)),
-        ],
+            pl.BlockSpec((LANES, width), lambda g, i: (first + g, 0)),
+        ]
+        + [pl.BlockSpec(memory_space=pl.ANY)] * len(held),
         out_specs=[
             row_columns,
             row_columns,
-            pl.BlockSpec((2, 1, rows, LANES), lambda g, i: (0, i, 0, g)),
+            pl.BlockSpec((2, 1, rows, LANES), lambda g, i: (0, i, 0, first + g)),
+            pl.BlockSpec((3, width, LANES), lambda g, i: (0, 0, first + g)),
+            pl.BlockSpec((LANES, width), lambda g, i: (first + g, 0)),
             pl.BlockSpec((SECTIONS, 2, 1, SUB, LANES), lambda g, i: (0, 0, i, 0, g)),
-            pl.BlockSpec((3, width, LANES), lambda g, i: (0, 0, g)),
-            pl.BlockSpec((LANES, width), lambda g, i: (g, 0)),
         ],
         out_shape=[
             jax.ShapeDtypeStruct((samples, rows, width), BF16),
             jax.ShapeDtypeStruct((samples, rows, width), BF16),
             jax.ShapeDtypeStruct((2, samples, rows, width), F32),
-            jax.ShapeDtypeStruct((SECTIONS, 2, samples, SUB, width), BF16),
             jax.ShapeDtypeStruct((3, width, width), BF16),
             jax.ShapeDtypeStruct((width, width), BF16),
-        ],
+            jax.ShapeDtypeStruct((SECTIONS, 2, samples, SUB, count * LANES), BF16),
+        ],
+        input_output_aliases={8 + i: i for i in range(len(held))},
         scratch_shapes=[pltpu.VMEM((keys, width), BF16)]
         + [pltpu.VMEM((LANES, width), F32)] * 4,
-        compiler_params=pltpu.CompilerParams(vmem_limit_bytes=48 << 20),
+        cost_estimate=pl.CostEstimate(
+            flops=count * samples * (24 * rows * keys * LANES + 14 * rows * width * LANES),
+            bytes_accessed=16 << 20,
+            transcendentals=count * samples * rows * keys * 2,
+        ),
         name="attend",
-    )(masks, tokens, arrived, cotangent, w_query, w_key, w_value, w_out)
+    )(masks, tokens, arrived, cotangent, w_query, w_key, w_value, w_out, *held)
 
 
 def toward(bit):
@@ -204,7 +218,7 @@
 
 
 def fetch(levels, choice, tokens):
-    samples, rows, width = tokens.shape
+    samples, _, width = tokens.shape
     vmem = pl.BlockSpec(memory_space=pltpu.VMEM)
     size = (SECTIONS, samples, SUB, width)
     sems = pltpu.SemaphoreType.DMA((SECTIONS,))
@@ -312,21 +326,23 @@
         + [pltpu.VMEM(stack, BF16)] * 3
         + [four, four, steps, steps, steps, steps],
         compiler_params=pltpu.CompilerParams(
-            collective_id=1, has_side_effects=True, vmem_limit_bytes=48 << 20
+            collective_id=1, has_side_effects=True
         ),
         name="settle",
     )(part, gw, go)
 
 
 def finish_kernel(
-    start_ref, own_ref, ret_ref, ctx_ref, dq_ref, wq_ref, wk_ref, wv_ref, wo_ref, sum_ref,
+    start_ref, own_ref, early_ref, late_ref, ctx_ref, dq_ref, wq_ref, wk_ref, wv_ref, wo_ref, sum_ref,
     out_ref, gtok_ref, gq_ref, gk_ref, gv_ref, go_ref, key_grads,
 ):
     out_ref[0] = mm(ctx_ref[0], wo_ref[...]).astype(BF16)
     key_grads[...] = own_ref[:, 0]
     for s in range(SECTIONS):
         at = pl.ds(pl.multiple_of(start_ref[s], SUB), SUB)
-        key_grads[:, at, :] += ret_ref[s, :, 0].astype(F32)
+        cut = early_ref.shape[-1]
+        key_grads[:, at, :cut] += early_ref[s, :, 0].astype(F32)
+        key_grads[:, at, cut:] += late_ref[s, :, 0].astype(F32)
     gtok_ref[0] = (
         nt(dq_ref[0], wq_ref[...])
         + nt(key_grads[0].astype(BF16), wk_ref[...])
@@ -336,7 +352,7 @@
         ref[...] = sum_ref[i].astype(F32)
 
 
-def finish(starts, own, ret, ctx, dq, w_query, w_key, w_value, w_out, sums):
+def finish(starts, own, early, late, ctx, dq, w_query, w_key, w_value, w_out, sums):
     samples, rows, width = ctx.shape
     row = pl.BlockSpec((1, rows, width), lambda i: (i, 0, 0))
     weight = pl.BlockSpec((width, width), lambda i: (0, 0))
@@ -348,7 +364,8 @@
         in_specs=[
             pl.BlockSpec(memory_space=pltpu.SMEM),
             pl.BlockSpec((2, 1, rows, width), lambda i: (0, i, 0, 0)),
-            pl.BlockSpec((SECTIONS, 2, 1, SUB, width), lambda i: (0, 0, i, 0, 0)),
+            pl.BlockSpec((SECTIONS, 2, 1, SUB, early.shape[-1]), lambda i: (0, 0, i, 0, 0)),
+            pl.BlockSpec((SECTIONS, 2, 1, SUB, late.shape[-1]), lambda i: (0, 0, i, 0, 0)),
             row, row, weight, weight, weight, weight,
             pl.BlockSpec((4, share, width), lambda i: (0, i, 0)),
         ],
@@ -356,9 +373,8 @@
         out_shape=[jax.ShapeDtypeStruct(ctx.shape, BF16)] * 2
         + [jax.ShapeDtypeStruct((width, width), F32)] * 4,
         scratch_shapes=[pltpu.VMEM((2, rows, width), F32)],
-        compiler_params=pltpu.CompilerParams(vmem_limit_bytes=48 << 20),
         name="finish",
-    )(starts, own, ret, ctx, dq, w_query, w_key, w_value, w_out, sums)
+    )(starts, own, early, late, ctx, dq, w_query, w_key, w_value, w_out, sums)
 
 
 def per_device(tokens, w_query, w_key, w_value, w_out, partner_block, head_masks, cotangent):
@@ -367,13 +383,18 @@
     head_width = width // head_masks.shape[2]
     choice = jnp.broadcast_to(partner_block[0][:, None, None], (SECTIONS, 8, LANES))
     arrived, theirs = fetch(levels, choice, tokens)
-    ctx, dq, own, part, gw, go = attend(
-        head_width, head_masks, tokens, arrived, cotangent, w_query, w_key, w_value, w_out
-    )
-    ret, sums = settle(levels, part, gw, go)
+    groups = width // LANES
+    inputs = (head_masks, tokens, arrived, cotangent, w_query, w_key, w_value, w_out)
+    *held, part = attend(head_width, 0, groups - LATE, (), *inputs)
+    early = []
+    for s in range(SECTIONS):
+        early.append(partner(part[s], "tok", levels - SECTIONS + s))
+    ctx, dq, own, gw, go, part = attend(head_width, groups - LATE, LATE, tuple(held), *inputs)
+    late, sums = settle(levels, part, gw, go)
     starts = theirs[:, 0, 0] * SUB
     return finish(
-        starts, own, ret, ctx, dq, w_query, w_key, w_value, w_out, sums.reshape(4, width, width)
+        starts, own, jnp.stack(early), late, ctx, dq, w_query, w_key, w_value, w_out,
+        sums.reshape(4, width, width),
     )
 
 

time: 156 us -> 141 us (0.904)
  Pallas kernels: 144 us -> 129 us
  local copies, waits for them, and re-layouts: 10.1 us -> 2.87 us
  starting transfers between devices: 0 us -> 4.19 us
  other arithmetic: 0.88 us -> 2.81 us
    pallas_call x1, Pallas kernels: 67.6 us -> 48.9 us  [settle(): pl.pallas_call(functools.partial(settle_kernel, levels), in_specs=[vmem]...]
    unnamed x24 -> x0, local copies, waits for them, and re-layouts: 8.81 us -> none
    ppermute x0 -> x4, starting transfers between devices: none -> 4.19 us  [partner(): lax.ppermute(x, axis, [(i, i ^ 1 << stride) for i in range(lax.axis_size(...]
    pallas_call x1 -> x2, Pallas kernels: 47.7 us -> 50.4 us  [attend(): pl.pallas_call(functools.partial(attend_kernel, head_width, scale, first,...]
  transfers between devices with their start and end apart: 0 -> 4, of which waited for: 0 -> 0; matrix products, arithmetic and copies ran while one was open for 0% -> 1% of each run, Pallas kernels for 0% -> 45%
where the time goes in v3:
time: 141 us; the launch traced here: 140 us
  Pallas kernels  129 us (91%)
  starting transfers between devices  4.19 us (3%)
  local copies, waits for them, and re-layouts  2.87 us (2%)
  other arithmetic  2.81 us (2%)
    pallas_call x2, Pallas kernels, attend(): pl.pallas_call(functools.partial(attend_kernel, head_width, scale, first,...  50.4 us
    pallas_call x1, Pallas kernels, settle(): pl.pallas_call(functools.partial(settle_kernel, levels), in_specs=[vmem]...  48.9 us
    pallas_call x1, Pallas kernels, fetch(): pl.pallas_call(functools.partial(fetch_kernel, levels), in_specs=[vmem, v...  22.1 us
    pallas_call x1, Pallas kernels, finish(): pl.pallas_call(finish_kernel, grid=(samples,), in_specs=[pl.BlockSpec(mem...  7.72 us
    ppermute x4, starting transfers between devices, partner(): lax.ppermute(x, axis, [(i, i ^ 1 << stride) for i in range(lax.axis_size(...  4.19 us
  transfers between devices with their start and end apart: 4, of which 0 were waited for; matrix products, arithmetic and copies ran while one was open for 1% of the time, Pallas kernels for 45%

profile of v3, /device:TPU:0, one launch (start us, length us, event | category | flops | bytes accessed | tf_op | source)
XLA Modules:
  0.0 139.8 jit_solution(16112781165515484751)
XLA Ops:
  0.6 1.3 broadcast_in_dim.8.choice_ref
  2.0 22.1 %fetch.1 = (bf16[4,2,128,512]{3,2,1,0:T(8,128)(2,1)}, s32[4,8,128]{2,1,0:T(8,128)}) custom-call(s32[4,8,128]{2,1,0:T(8,128)} %broadcast_in_dim.8.choice_ref, bf16[2,512,512]{2,1,0:T(8,128)(2,1)} %tok_ref.5), custom_call_target="tpu_custom_call" | custom-call | tf_op jit(solution)/shard_map/fetch/pallas_call | solution.py:225
  24.0 36.4 %attend.2 = (bf16[2,512,512]{2,1,0:T(8,128)(2,1)}, bf16[2,512,512]{2,1,0:T(8,128)(2,1)}, f32[2,2,512,512]{3,2,1,0:T(8,128)}, bf16[3,512,512]{2,1,0:T(8,128)(2,1)...) custom-call(s32[1,4,8]{2,1,0:T(4,128)} %mask_ref.3, bf16[2,512,512]{2,1,0:T(8,128)(2,1)} %tok_ref.5, ...), custom_call_target="tpu_custom_call" | custom-call | flops 12482248704 | bytes 16777216 | tf_op jit(solution)/shard_map/attend/pallas_call | solution.py:126
  60.5 1.5 %slice_bitcast_fusion.3 = (bf16[2,2,128,384]{3,2,1,0:T(8,128)(2,1)S(1)}, bf16[2,2,128,384]{3,2,1,0:T(8,128)(2,1)S(1)}, bf16[2,2,128,384]{3,2,1,0:T(8,128)(2,1)S(1)}, bf16[2,2,128,384]{3,2,1,0:T(8,128)(2,1)S(1)}) fusion(bf16[4,2,2,128,384]{4,3,2,1,0:T(8,128)(2,1)} %get-tuple-element.30), kind=kLoop, calls=%fused_computation.4 | loop fusion | bytes 3145728 | tf_op jit(solution)/shard_map/squeeze | solution.py:391
  62.0 0.1 collective-permute-start
  62.1 1.7 %collective-permute-start.3 = (bf16[2,2,128,384]{3,2,1,0:T(8,128)(2,1)S(1)}, bf16[2,2,128,384]{3,2,1,0:T(8,128)(2,1)S(1)}, u32[]{:S(2)}, u32[]{:S(2)}) collective-permute-start(bf16[2,2,128,384]{3,2,1,0:T(8,128)(2,1)S(1)} %get-tuple-element.39), channel_id=1, source_target_pairs={{0,8},{1,9},{2,10},{3,11},{4,12},{5,13},{6,14},{7,15},{8,0},{9,1},... | collective-permute-start | bytes 1179656 | tf_op jit(solution)/shard_map/ppermute | solution.py:22
  63.8 1.4 %collective-permute-start.2 = (bf16[2,2,128,384]{3,2,1,0:T(8,128)(2,1)S(1)}, bf16[2,2,128,384]{3,2,1,0:T(8,128)(2,1)S(1)}, u32[]{:S(2)}, u32[]{:S(2)}) collective-permute-start(bf16[2,2,128,384]{3,2,1,0:T(8,128)(2,1)S(1)} %get-tuple-element.40), channel_id=1, source_target_pairs={{0,4},{1,5},{2,6},{3,7},{4,0},{5,1},{6,2},{7,3},{8,12},{9,13},{10,... | collective-permute-start | bytes 1179656 | tf_op jit(solution)/shard_map/ppermute | solution.py:22
  65.2 1.1 collective-permute-start.1
  66.2 14.0 %attend.3 = (bf16[2,512,512]{2,1,0:T(8,128)(2,1)}, bf16[2,512,512]{2,1,0:T(8,128)(2,1)}, f32[2,2,512,512]{3,2,1,0:T(8,128)}, bf16[3,512,512]{2,1,0:T(8,128)(2,1)...) custom-call(s32[1,4,8]{2,1,0:T(4,128)} %mask_ref.3, ...), custom_call_target="tpu_custom_call", output_to_operand_aliasing={{0}: (8, {}), {1}: (9, {}), {2}: (10, {}), {3}: (11, {}), {... | custom-call | flops 4160749568 | bytes 16777216 | tf_op jit(solution)/shard_map/attend/pallas_call | solution.py:126
  80.2 48.9 %settle.1 = (bf16[4,2,2,128,128]{4,3,2,1,0:T(8,128)(2,1)}, bf16[2048,512]{1,0:T(8,128)(2,1)}) custom-call(bf16[4,2,2,128,128]{4,3,2,1,0:T(8,128)(2,1)} %get-tuple-element.31.part_ref, bf16[3,512,512]{2,1,0:T(8,128)(2,1)} %get-tuple-element.32.gw_ref, bf16[512,512]{1,0:T(8,128)(2,1)} %get-tuple-element.33.go_ref), custom_call_target="tpu_custom_call" | custom-call | tf_op jit(solution)/shard_map/settle/pallas_call | solution.py:317
  129.1 1.4 %multiply_reduce_fusion.start_ref = s32[4]{0:T(128)} fusion(s32[4,8,128]{2,1,0:T(8,128)} %get-tuple-element.22), kind=kLoop, calls=%fused_computation.5 | loop fusion | flops 4 | bytes 32 | tf_op jit(solution)/shard_map/mul | solution.py:394
  130.5 0.0 collective-permute-done
  130.5 0.0 collective-permute-done.3
  130.5 0.0 collective-permute-done.2
  130.5 0.0 collective-permute-done.1
  130.5 1.4 pad_maximum_fusion.early_ref
  131.9 7.7 %finish.1 = (bf16[2,512,512]{2,1,0:T(8,128)(2,1)}, bf16[2,512,512]{2,1,0:T(8,128)(2,1)}, f32[512,512]{1,0:T(8,128)}, f32[512,512]{1,0:T(8,128)}, f32[512,512]{1,0:T(8,128)}, /*index=5*/f32[512,512]{1,0:T(8,128)}) custom-call(s32[4]{0:T(128)} %multiply_reduce_fusion.start_ref, f32[2,2,512,512]{3,2,1,0:T(8,128)} %get-tuple-element.29.own_ref, ...), custom_call_target="tpu_custom_call" | custom-call | tf_op jit(solution)/shard_map/finish/pallas_call | solution.py:361
Async XLA Ops:
  62.0 68.5 %collective-permute-start = (bf16[2,2,128,384]{3,2,1,0:T(8,128)(2,1)S(1)}, bf16[2,2,128,384]{3,2,1,0:T(8,128)(2,1)S(1)}, u32[]{:S(2)}, u32[]{:S(2)}) collective-permute-start(bf16[2,2,128,384]{3,2,1,0:T(8,128)(2,1)S(1)} %get-tuple-element.38), channel_id=1, source_target_pairs={{0,1},{1,0},{2,3},{3,2},{4,5},{5,4},{6,7},{7,6},{8,9},{9,8},{10,11... | collective-permute-start | bytes 1179656 | tf_op jit(solution)/shard_map/ppermute | solution.py:22
  62.1 68.4 %collective-permute-start.3 = (bf16[2,2,128,384]{3,2,1,0:T(8,128)(2,1)S(1)}, bf16[2,2,128,384]{3,2,1,0:T(8,128)(2,1)S(1)}, u32[]{:S(2)}, u32[]{:S(2)}) collective-permute-start(bf16[2,2,128,384]{3,2,1,0:T(8,128)(2,1)S(1)} %get-tuple-element.39), channel_id=1, source_target_pairs={{0,8},{1,9},{2,10},{3,11},{4,12},{5,13},{6,14},{7,15},{8,0},{9,1},... | collective-permute-start | bytes 1179656 | tf_op jit(solution)/shard_map/ppermute | solution.py:22
  63.8 66.7 %collective-permute-start.2 = (bf16[2,2,128,384]{3,2,1,0:T(8,128)(2,1)S(1)}, bf16[2,2,128,384]{3,2,1,0:T(8,128)(2,1)S(1)}, u32[]{:S(2)}, u32[]{:S(2)}) collective-permute-start(bf16[2,2,128,384]{3,2,1,0:T(8,128)(2,1)S(1)} %get-tuple-element.40), channel_id=1, source_target_pairs={{0,4},{1,5},{2,6},{3,7},{4,0},{5,1},{6,2},{7,3},{8,12},{9,13},{10,... | collective-permute-start | bytes 1179656 | tf_op jit(solution)/shard_map/ppermute | solution.py:22
  65.2 65.3 %collective-permute-start.1 = (bf16[2,2,128,384]{3,2,1,0:T(8,128)(2,1)S(1)}, bf16[2,2,128,384]{3,2,1,0:T(8,128)(2,1)S(1)}, u32[]{:S(2)}, u32[]{:S(2)}) collective-permute-start(bf16[2,2,128,384]{3,2,1,0:T(8,128)(2,1)S(1)} %get-tuple-element.41), channel_id=1, source_target_pairs={{0,2},{1,3},{2,0},{3,1},{4,6},{5,7},{6,4},{7,5},{8,10},{9,11},{10,... | collective-permute-start | bytes 1179656 | tf_op jit(solution)/shard_map/ppermute | solution.py:22
